TPU v7x, 32 devices: a whole 2x2x4 slice. The times are simulated.
32 devices in a mesh: rows: 2 (over x), cols: 2 (over core), imgs: 8 (over z, y).
Axes of the slice: x: 2, y: 2, z: 4, core: 2. Of those that a mesh axis runs over, the one named last changes fastest.
Arguments:
- patches: bfloat16 [8, 30, 30, 768], P('imgs', 'rows', 'cols'), may hold values from -6 to 6
- patch_mask: int32 [8, 30, 30], P('imgs'), may hold values from 0 to 1, as said below
- norm1_gain: float32 [768], replicated, may hold values from 0.1 to 1.9
- norm1_shift: float32 [768], replicated, may hold values from -3 to 3
- qkv_weight: bfloat16 [768, 2304], replicated, may hold values from -0.21875 to 0.21875
- qv_bias: float32 [768, 2], replicated, may hold values from -3 to 3
- out_weight: bfloat16 [768, 768], replicated, may hold values from -1.25 to 1.25
- out_bias: float32 [768], replicated, may hold values from -3 to 3
- norm2_gain: float32 [768], replicated, may hold values from 0.1 to 1.9
- norm2_shift: float32 [768], replicated, may hold values from -3 to 3
- fc1_weight: bfloat16 [768, 3072], replicated, may hold values from -0.21875 to 0.21875
- fc1_bias: float32 [3072], replicated, may hold values from -3 to 3
- fc2_weight: bfloat16 [3072, 768], replicated, may hold values from -0.109375 to 0.109375
- fc2_bias: float32 [768], replicated, may hold values from -3 to 3
- cotangent: bfloat16 [8, 30, 30, 768], P('imgs', 'rows', 'cols'), may hold values from -6 to 6
Outputs:
- layer_out: bfloat16 [8, 30, 30, 768], P('imgs', 'rows', 'cols')
- patches_grad: bfloat16 [8, 30, 30, 768], P('imgs', 'rows', 'cols')
- norm1_gain_grad: float32 [768], P('imgs')
- norm1_shift_grad: float32 [768], P('imgs')
- qkv_weight_grad: float32 [768, 2304], P('imgs')
- qv_bias_grad: float32 [768, 2], P('imgs')
- out_weight_grad: float32 [768, 768], P('imgs')
- out_bias_grad: float32 [768], P('imgs')
- norm2_gain_grad: float32 [768], P('imgs')
- norm2_shift_grad: float32 [768], P('imgs')
- fc1_weight_grad: float32 [768, 3072], P('imgs')
- fc1_bias_grad: float32 [3072], P('imgs')
- fc2_weight_grad: float32 [3072, 768], P('imgs')
- fc2_bias_grad: float32 [768], P('imgs')
Inputs may be any that keep to these rules, and one draw needn't show every extreme that they name: For each image, patch_mask is 1 on a rectangle of h rows and w columns at the top left of the grid and 0 elsewhere, with 12 <= h, w <= 30; image 0 is whole and image 1 has h = w = 12.
All inputs are finite; a program needn't handle non-finite values.
Results may differ from a plain program's by a relative error of at most 0.012.
Values may be sent and summed in bfloat16 or wider, within the bound.
No kernel may reach another device: no remote copies, remote signals or barrier semaphores. Data moves between devices by JAX's collectives and lax.ppermute only.
A program may use at most 128 MiB of HBM per device.

v0:
```python
import functools

import jax
import jax.numpy as jnp
from jax import lax
from jax.experimental import pallas as pl
from jax.experimental.pallas import tpu as pltpu
from jax.sharding import PartitionSpec as P

HEADS = 12
NORM_EPS = 1e-06
MASKED_SCORE = -1e30
GROUP = ("rows", "cols")
BF = jnp.bfloat16
F32 = jnp.float32


def dot(left, right, dims):
    return lax.dot_general(left, right, (dims, ((), ())), preferred_element_type=F32)


def mm(left, right):
    return dot(left, right, ((1,), (0,)))


def mm_nt(left, right):
    return dot(left, right, ((1,), (1,)))


def mm_tn(left, right):
    return dot(left, right, ((0,), (0,)))


def to_peer(value, rel):
    if rel == 1:
        return lax.ppermute(value, "cols", [(0, 1), (1, 0)])
    if rel == 2:
        return lax.ppermute(value, "rows", [(0, 1), (1, 0)])
    return lax.ppermute(value, GROUP, [(i, i ^ 3) for i in range(4)])


def tie(values, others):
    flat, tree = jax.tree.flatten((values, others))
    return jax.tree.unflatten(tree, lax.optimization_barrier(flat))


def gather_tiles(value, others=()):
    across = to_peer(value, 2)
    beside = to_peer(value, 1)
    across, others = tie(across, others)
    return [value, beside, across, to_peer(across, 1)], others


def scatter_tiles(blocks):
    return [blocks[0], to_peer(blocks[1], 1), to_peer(blocks[2], 2), to_peer(blocks[3], 3)]


def norm_stats(values):
    mean_val = jnp.mean(values, axis=-1, keepdims=True)
    centred = values - mean_val
    var_val = jnp.mean(centred * centred, axis=-1, keepdims=True)
    inv = lax.rsqrt(var_val + NORM_EPS)
    return centred * inv, inv


def norm_back(grads, normed, inv, gain):
    g = grads * gain
    return (
        g
        - jnp.mean(g, axis=-1, keepdims=True)
        - normed * jnp.mean(g * normed, axis=-1, keepdims=True)
    ) * inv


def gelu_parts(x):
    cdf = 0.5 * (1.0 + lax.erf(x * 0.7071067811865476))
    pdf = jnp.exp(-0.5 * x * x) * 0.3989422804014327
    return x * cdf, cdf + x * pdf


def exchange_near(parts):
    side = lax.axis_index("imgs") % 2
    count = lax.axis_size("imgs")
    send = lax.dynamic_index_in_dim(parts, 1 - side, 1, keepdims=False)
    keep = lax.dynamic_index_in_dim(parts, side, 1, keepdims=False)
    return keep, lax.ppermute(send, "imgs", [(i, i ^ 1) for i in range(count)])


def exchange_far(parts):
    count = lax.axis_size("imgs")
    place = lax.axis_index("imgs") // 2
    got = [lax.dynamic_index_in_dim(parts, place, 0, keepdims=False)]
    for k in range(count // 2 - 1, 0, -1):
        send = lax.dynamic_index_in_dim(parts, place ^ k, 0, keepdims=False)
        got.append(lax.ppermute(send, "imgs", [(i, i ^ (2 * k)) for i in range(count)]))
    return got


def total_of(blocks):
    return functools.reduce(jnp.add, [b.astype(F32) for b in blocks])


def direct_sum(imgs):
    return imgs <= 8 and imgs & (imgs - 1) == 0


def plain_sum(parts):
    return lax.psum_scatter(parts, "imgs", scatter_dimension=0, tiled=False)


def own_order(blocks, tile):
    stacked = jnp.stack(blocks)
    return [lax.dynamic_index_in_dim(stacked, tile ^ k, 0, keepdims=False) for k in range(4)]


SMEM = pl.BlockSpec(memory_space=pltpu.SMEM)
VMEM = pl.BlockSpec(memory_space=pltpu.VMEM)
PAD = 16


def vec_call(kernel, outs, n_in, scratch=(), us=5):
    return pl.pallas_call(
        kernel,
        out_shape=outs,
        in_specs=[SMEM] + [VMEM] * n_in,
        out_specs=jax.tree.map(lambda _: VMEM, outs),
        scratch_shapes=list(scratch),
        cost_estimate=cost(us),
    )


def cost(us):
    return pl.CostEstimate(flops=us * 10**9, transcendentals=0, bytes_accessed=us * 10**6)


def sds(shape, dtype=BF):
    return jax.ShapeDtypeStruct(shape, dtype)


def load_tile(ref, scratch, at):
    rows, cols, width = ref.shape[1:]
    scratch[at : at + rows * PAD, :] = jnp.zeros((rows * PAD, width), scratch.dtype)
    for i in range(rows):
        scratch[at + i * PAD : at + i * PAD + cols, :] = ref[0, i]


def store_tile(ref, value):
    rows, cols, _ = ref.shape[1:]
    for i in range(rows):
        ref[0, i] = value[i * PAD : i * PAD + cols, :]


def mask_edges(mask):
    m = mask[0].astype(F32)
    high = jnp.sum(m[:, 0:1], axis=0, keepdims=True)
    wide = jnp.sum(m[0:1, :], axis=1, keepdims=True)
    return high, wide


def keep_tokens(edges, place, rows, cols, axis):
    toks = rows * PAD
    shape = (toks, 1) if axis == 0 else (1, toks)
    tok = lax.broadcasted_iota(jnp.int32, shape, axis)
    c = tok & (PAD - 1)
    r = ((tok >> 4) + (place >> 1) * rows).astype(F32)
    at = (c + (place & 1) * cols).astype(F32)
    ok = (c < cols) & (r < edges[0]) & (at < edges[1])
    return jnp.where(ok, 1.0, 0.0).astype(F32)


def mask_row(tile, mask, rows, cols):
    edges = mask_edges(mask)
    keep = [keep_tokens(edges, tile[0] ^ r, rows, cols, 1) for r in range(4)]
    return jnp.where(jnp.concatenate(keep, axis=1) > 0, 0.0, MASKED_SCORE).astype(F32)


def vec_row(ref):
    return ref[...].reshape(1, -1)


def heads_kernel(tile, qkv_w, qv_b, w_own, b_own):
    width = qv_b.shape[1]
    part = width // 4
    for g in range(4):

        @pl.when(tile[0] == g)
        def _():
            for i in range(3):
                src = i * width + g * part
                w_own[:, i * part : (i + 1) * part] = qkv_w[:, src : src + part]
            b_own[:, :part] = qv_b[0:1, g * part : (g + 1) * part]
            b_own[:, part : 2 * part] = jnp.zeros((1, part), F32)
            b_own[:, 2 * part :] = qv_b[1:2, g * part : (g + 1) * part]


def units_kernel(tile, fc1, fc1_b, fc1_own, fc1_b_own, *, quarter):
    for g in range(4):

        @pl.when(tile[0] == g)
        def _():
            for i in range(fc1.shape[1] // (4 * quarter)):
                src = (4 * i + g) * quarter
                dst = i * quarter
                fc1_own[:, dst : dst + quarter] = fc1[:, src : src + quarter]
                fc1_b_own[:, dst : dst + quarter] = fc1_b[:, src : src + quarter]


def attn_kernel(
    tile, mask, x0, x1, x2, x3, gain, shift, w, bias, hid, nrm, qkv, lse, c0, c1, c2, c3, xs, ctx
):
    rows, cols, width = x0.shape[1:]
    toks = rows * PAD
    part = w.shape[1] // 3
    dim = width // HEADS
    scale = dim ** (-0.5)
    for r, ref in enumerate((x0, x1, x2, x3)):
        load_tile(ref, xs, r * toks)

    normed, _ = norm_stats(xs[...].astype(F32))
    nrm[...] = normed.astype(BF)
    hid[...] = (normed * vec_row(gain) + vec_row(shift)).astype(BF)
    qkv[...] = (mm(hid[...], w[...]) + bias[...]).astype(BF)
    masked = mask_row(tile, mask, rows, cols)

    def attend(r, carry):
        at = pl.ds(pl.multiple_of(r * toks, toks), toks)
        outs = []
        for h in range(part // dim):
            q = qkv[at, h * dim : (h + 1) * dim]
            k = qkv[:, part + h * dim : part + (h + 1) * dim]
            v = qkv[:, 2 * part + h * dim : 2 * part + (h + 1) * dim]
            s = mm_nt(q * scale, k) + masked
            top = jnp.max(s, axis=-1, keepdims=True)
            e = jnp.exp(s - top)
            total = jnp.sum(e, axis=-1, keepdims=True)
            outs.append((mm(e.astype(BF), v) * (1.0 / total)).astype(BF))
            lse[at, h : h + 1] = top + jnp.log(total)
        ctx[r] = jnp.concatenate(outs, axis=1)
        return carry

    lax.fori_loop(0, 4, attend, 0)
    for r, ref in enumerate((c0, c1, c2, c3)):
        ref[...] = ctx[r]


def branch_kernel(tile, c0, c1, c2, c3, wo, bo, x, gain, shift, resid, hid, xs):
    part = c0.shape[1]
    load_tile(x, xs, 0)
    acc = xs[...].astype(F32) + vec_row(bo)
    for r, ref in enumerate((c0, c1, c2, c3)):
        at = pl.multiple_of((tile[0] ^ r) * part, part)
        acc = acc + mm(ref[...], wo[pl.ds(at, part), :])
    resid[...] = acc
    normed, _ = norm_stats(acc)
    hid[...] = (normed * vec_row(gain) + vec_row(shift)).astype(BF)


def mlp_kernel(
    tile, mask, resid, hid, ct, gain, fc1, fc1_b, fc2, fc2_b, out, branch, rgrad, vecs, up, acc, nacc
):
    step = pl.program_id(0)
    rows, cols, _ = ct.shape[1:]

    @pl.when(step == 0)
    def _():
        load_tile(ct, up, 0)
        up[...] = (up[...].astype(F32) * keep_tokens(mask_edges(mask), tile[0], rows, cols, 0)).astype(BF)
        acc[...] = jnp.zeros_like(acc)
        nacc[...] = jnp.zeros_like(nacc)

    act, dgelu = gelu_parts(mm(hid[...], fc1[...]) + fc1_b[...])
    acc[...] += mm(act.astype(BF), fc2[...])
    inner = (mm_nt(up[...], fc2[...]) * dgelu).astype(BF)
    nacc[...] += mm_nt(inner, fc1[...])

    @pl.when(step == pl.num_programs(0) - 1)
    def _():
        res = resid[...]
        keep = keep_tokens(mask_edges(mask), tile[0], rows, cols, 0)
        store_tile(out, (keep * (res + acc[...] + vec_row(fc2_b))).astype(BF))
        normed, inv = norm_stats(res)
        n = nacc[...]
        vecs[0:1, :] = jnp.sum(n * normed, axis=0, keepdims=True)
        vecs[1:2, :] = jnp.sum(n, axis=0, keepdims=True)
        grad = up[...].astype(F32) + norm_back(n, normed, inv, vec_row(gain))
        rgrad[...] = grad
        branch[...] = grad.astype(BF)


def ffgrad_kernel(
    tile, mask, h0, h1, h2, h3, t0, t1, t2, t3, fc1, fc1_b, fc2, g1, g2, b1, b2, up, a1, a2
):
    rows, cols, _ = t0.shape[1:]
    edges = mask_edges(mask)
    hids = (h0, h1, h2, h3)
    for r, ref in enumerate((t0, t1, t2, t3)):
        load_tile(ref, up, 0)
        wide = up[...].astype(F32) * keep_tokens(edges, tile[0] ^ r, rows, cols, 0)
        low = wide.astype(BF)
        h = hids[r][...]
        act, dgelu = gelu_parts(mm(h, fc1[...]) + fc1_b[...])
        inner = (mm_nt(low, fc2[...]) * dgelu).astype(BF)
        d1 = mm_tn(h, inner)
        d2 = mm_tn(act.astype(BF), low)
        s1 = jnp.sum(inner.astype(F32), axis=0, keepdims=True)
        s2 = jnp.sum(wide, axis=0, keepdims=True)
        if r == 0:
            a1[...], a2[...], b1[...], b2[...] = d1, d2, s1, s2
        elif r < 3:
            a1[...] += d1
            a2[...] += d2
            b1[...] += s1
            b2[...] += s2
        else:
            g1[...] = (a1[...] + d1).astype(BF)
            g2[...] = (a2[...] + d2).astype(BF)
            b1[...] += s1
            b2[...] += s2


def outgrad_kernel(tile, b0, b1, b2, b3, wo, c0, c1, c2, c3, dctx, gout, bsum):
    toks, part = c0.shape
    at = pl.multiple_of(tile[0] * part, part)
    w = wo[pl.ds(at, part), :]
    ctx = (c0, c1, c2, c3)
    acc = None
    total = None
    for r, ref in enumerate((b0, b1, b2, b3)):
        low = ref[...]
        dctx[r * toks : (r + 1) * toks, :] = mm_nt(low, w).astype(BF)
        d = mm_tn(ctx[r][...], low)
        s = jnp.sum(low.astype(F32), axis=0, keepdims=True)
        acc = d if r == 0 else acc + d
        total = s if r == 0 else total + s
    gout[...] = acc.astype(BF)
    bsum[...] = total


def attnback_kernel(
    tile,
    mask,
    dctx,
    qkv,
    lse,
    hid,
    nrm,
    w,
    bsum,
    vec2,
    fb2,
    m0,
    m1,
    m2,
    m3,
    gqkv,
    vecs,
    dk,
    dv,
    mix,
    *,
    cols,
):
    total, three = qkv.shape
    part = three // 3
    toks = total // 4
    dim = hid.shape[1] // HEADS
    rows = toks // PAD
    scale = dim ** (-0.5)
    masked = mask_row(tile, mask, rows, cols)
    dk[...] = jnp.zeros_like(dk)
    dv[...] = jnp.zeros_like(dv)

    def attend(r, carry):
        at = pl.ds(pl.multiple_of(r * toks, toks), toks)
        dqs = []
        q_all = qkv[at, :part] * scale
        do_all = dctx[at, :]
        q_turned = q_all.T
        do_turned = do_all.T
        for h in range(part // dim):
            at_h = slice(h * dim, (h + 1) * dim)
            k = qkv[:, part + h * dim : part + (h + 1) * dim]
            v = qkv[:, 2 * part + h * dim : 2 * part + (h + 1) * dim]
            p = jnp.exp(mm_nt(q_all[:, at_h], k) + masked - lse[at, h : h + 1])
            dp = mm_nt(do_all[:, at_h], v)
            ds = (p * (dp - jnp.sum(dp * p, axis=-1, keepdims=True))).astype(BF)
            dqs.append((mm(ds, k) * scale).astype(BF))
            dv[at_h, :] += mm(do_turned[at_h], p.astype(BF))
            dk[at_h, :] += mm(q_turned[at_h], ds)
        mix[at, :part] = jnp.concatenate(dqs, axis=1)
        return carry

    lax.fori_loop(0, 4, attend, 0)
    mix[:, part : 2 * part] = dk[...].T.astype(BF)
    mix[:, 2 * part :] = dv[...].T.astype(BF)
    gqkv[...] = mm_tn(hid[...], mix[...]).astype(BF)
    for r, ref in enumerate((m0, m1, m2, m3)):
        ref[...] = mix[r * toks : (r + 1) * toks, :]
    col_sum = jnp.sum(mix[...].astype(F32), axis=0, keepdims=True)
    chunk = 256
    for i in range(w.shape[0] // chunk):
        at = slice(i * chunk, (i + 1) * chunk)
        n = mm_nt(mix[...], w[at, :])
        vecs[0:1, at] = jnp.sum(n * nrm[:, at].astype(F32), axis=0, keepdims=True)
        vecs[1:2, at] = jnp.sum(n, axis=0, keepdims=True)
    slot = lax.broadcasted_iota(jnp.int32, (1, 4 * part), 1)
    own = (slot >= tile[0] * part) & (slot < (tile[0] + 1) * part)
    lone = jnp.where(tile[0] == 0, 1.0, 0.0).astype(F32)
    for i in range(3):
        piece = col_sum[:, i * part : (i + 1) * part]
        vecs[2 + i : 3 + i, :] = jnp.where(own, jnp.concatenate([piece] * 4, axis=1), 0.0)
    vecs[5:6, :] = bsum[...] * lone
    vecs[6:8, :] = vec2[...]
    vecs[8:9, :] = fb2[...] * lone


def input_kernel(tile, m0, m1, m2, m3, w, x, rgrad, gain, out, ms, xs):
    part = m0.shape[1] // 3
    for r, ref in enumerate((m0, m1, m2, m3)):
        ms[r] = ref[...]
    tiles = [ms[tile[0] ^ g] for g in range(4)]
    full = jnp.concatenate(
        [m[:, i * part : (i + 1) * part] for i in range(3) for m in tiles], axis=1
    )
    n = mm_nt(full, w[...])
    load_tile(x, xs, 0)
    normed, inv = norm_stats(xs[...].astype(F32))
    store_tile(out, (rgrad[...] + norm_back(n, normed, inv, vec_row(gain))).astype(BF))


def ffout_kernel(tile, a0, a1, a2, a3, b0, b1, b2, b3, fc1, fc2, ps):
    quarter = fc2.shape[0] // 4
    for r, ref in enumerate((a0, a1, a2, a3)):
        ps[r] = ref[...].astype(F32)
    for g in range(4):
        piece = ps[tile[0] ^ g]
        for i in range(fc1.shape[1] // (4 * quarter)):
            dst = (4 * i + g) * quarter
            fc1[:, dst : dst + quarter] = piece[:, i * quarter : (i + 1) * quarter]
    for r, ref in enumerate((b0, b1, b2, b3)):
        ps[r, :quarter, :] = ref[...].astype(F32)
    for g in range(4):
        fc2[g * quarter : (g + 1) * quarter, :] = ps[tile[0] ^ g][:quarter]


def attnout_kernel(
    tile, p0, p1, p2, p3, gqkv, gout, v0, v1, v5, v6, v7, v8, qv, units, ps
):
    rows, width = gout.shape
    part = width // 4
    quarter = units.shape[0] // 4
    height = ps.shape[1] - rows
    for r, ref in enumerate((p0, p1, p2, p3)):
        ps[r] = ref[...].astype(F32)
    total = None
    tails = []
    for g in range(4):
        piece = ps[tile[0] ^ g]
        for i in range(3):
            dst = i * width + g * part
            gqkv[:, dst : dst + part] = piece[:rows, i * part : (i + 1) * part]
        gout[:, g * part : (g + 1) * part] = piece[:rows, 3 * part :]
        tail = jnp.concatenate([piece[rows + j : rows + j + 1] for j in range(height)], axis=1)
        total = tail if g == 0 else total + tail
        tails.append(tail[:, 9 * rows : 9 * rows + quarter])
    for i, ref in ((0, v0), (1, v1), (5, v5), (6, v6), (7, v7), (8, v8)):
        ref[...] = total[0, i * rows : (i + 1) * rows]
    both = [total[:, i * rows : (i + 1) * rows] for i in (2, 4)]
    qv[...] = jnp.concatenate(both, axis=0).T
    units[...] = jnp.concatenate(tails, axis=1)[0]


def layer(
    patches,
    patch_mask,
    norm1_gain,
    norm1_shift,
    qkv_weight,
    qv_bias,
    out_weight,
    out_bias,
    norm2_gain,
    norm2_shift,
    fc1_weight,
    fc1_bias,
    fc2_weight,
    fc2_bias,
    cotangent,
):
    _, rows, cols, width = patches.shape
    ff = fc1_weight.shape[1]
    imgs = lax.axis_size("imgs")
    part = width // 4
    units = ff // 4
    quarter = units // imgs
    share = width // imgs
    toks = rows * PAD
    total = 4 * toks
    tile = lax.axis_index("rows") * 2 + lax.axis_index("cols")
    at_tile = tile.reshape(1).astype(jnp.int32)

    def row(v):
        return v.reshape(1, -1)

    steps = 4
    w_own, b_own = pl.pallas_call(
        heads_kernel,
        grid=(steps,),
        in_specs=[
            SMEM,
            pl.BlockSpec((width // steps, 3 * width), lambda i: (i, 0)),
            pl.BlockSpec((2, width), lambda i: (0, 0)),
        ],
        out_specs=[
            pl.BlockSpec((width // steps, 3 * part), lambda i: (i, 0)),
            pl.BlockSpec((1, 3 * part), lambda i: (0, 0)),
        ],
        out_shape=[sds((width, 3 * part)), sds((1, 3 * part), F32)],
        cost_estimate=cost(4),
        name="heads",
    )(at_tile, qkv_weight, qv_bias.T)
    fc1_own, fc1_b_own = pl.pallas_call(
        functools.partial(units_kernel, quarter=quarter),
        grid=(steps,),
        in_specs=[
            SMEM,
            pl.BlockSpec((width // steps, ff), lambda i: (i, 0)),
            pl.BlockSpec((1, ff), lambda i: (0, 0)),
        ],
        out_specs=[
            pl.BlockSpec((width // steps, units), lambda i: (i, 0)),
            pl.BlockSpec((1, units), lambda i: (0, 0)),
        ],
        out_shape=[sds((width, units)), sds((1, units), F32)],
        cost_estimate=cost(4),
        name="units",
    )(at_tile, fc1_weight, row(fc1_bias))
    x_blocks, (w_own, b_own, fc1_own) = gather_tiles(patches, (w_own, b_own, fc1_own))

    hid1, nrm1, qkv, lse, *ctx = vec_call(
        attn_kernel,
        [
            sds((total, width)),
            sds((total, width)),
            sds((total, 3 * part)),
            sds((total, 128), F32),
        ]
        + [sds((toks, part))] * 4,
        9,
        [pltpu.VMEM((total, width), BF), pltpu.VMEM((4, toks, part), BF)],
        us=13,
    )(at_tile, patch_mask, *x_blocks, norm1_gain, norm1_shift, w_own, b_own)
    ct_blocks, ctx = gather_tiles(cotangent, ctx)
    later_tile, _ = tie(at_tile, ctx)

    fc2_own = lax.dynamic_index_in_dim(
        fc2_weight.reshape(imgs, 4, quarter, width), later_tile[0], 1, keepdims=False
    ).reshape(units, width)

    ctx_in = scatter_tiles(ctx)
    ctx_in, (fc2_own,) = tie(ctx_in, (fc2_own,))
    resid, hid2 = vec_call(
        branch_kernel,
        [sds((toks, width), F32), sds((toks, width))],
        9,
        [pltpu.VMEM((toks, width), BF)],
        us=3,
    )(at_tile, *ctx_in, out_weight, out_bias, patches, norm2_gain, norm2_shift)

    chunks = 4
    step = ff // chunks

    def whole(*shape):
        return pl.BlockSpec(shape, lambda i: (0,) * len(shape))

    layer_out, branch, rgrad, vec2 = pl.pallas_call(
        mlp_kernel,
        grid=(chunks,),
        in_specs=[
            SMEM,
            whole(*patch_mask.shape),
            whole(toks, width),
            whole(toks, width),
            whole(1, rows, cols, width),
            whole(width),
            pl.BlockSpec((width, step), lambda i: (0, i)),
            pl.BlockSpec((1, step), lambda i: (0, i)),
            pl.BlockSpec((step, width), lambda i: (i, 0)),
            whole(width),
        ],
        out_specs=[
            whole(1, rows, cols, width),
            whole(toks, width),
            whole(toks, width),
            whole(2, width),
        ],
        out_shape=[
            sds((1, rows, cols, width)),
            sds((toks, width)),
            sds((toks, width), F32),
            sds((2, width), F32),
        ],
        scratch_shapes=[
            pltpu.VMEM((toks, width), BF),
            pltpu.VMEM((toks, width), F32),
            pltpu.VMEM((toks, width), F32),
        ],
        cost_estimate=cost(11),
        name="mlp",
    )(
        at_tile,
        patch_mask,
        resid,
        hid2,
        cotangent,
        norm2_gain,
        fc1_weight,
        row(fc1_bias),
        fc2_weight,
        fc2_bias,
    )
    hid2_blocks, (branch,) = gather_tiles(hid2, (branch,))

    g1, g2, fb1, fb2 = vec_call(
        ffgrad_kernel,
        [sds((width, units)), sds((units, width)), sds((1, units), F32), sds((1, width), F32)],
        12,
        [
            pltpu.VMEM((toks, width), BF),
            pltpu.VMEM((width, units), F32),
            pltpu.VMEM((units, width), F32),
        ],
        us=9,
    )(at_tile, patch_mask, *hid2_blocks, *ct_blocks, fc1_own, fc1_b_own, fc2_own)
    branch_blocks, (g1, g2) = gather_tiles(branch, (g1, g2))

    dctx, gout, bsum = vec_call(
        outgrad_kernel,
        [sds((total, part)), sds((part, width)), sds((1, width), F32)],
        9,
        us=4,
    )(at_tile, *branch_blocks, out_weight, *ctx)
    direct = direct_sum(imgs)
    (g1, g2), (gout,) = tie((g1, g2), (gout,))
    g1 = g1.reshape(imgs, share, units)
    g2 = g2.reshape(imgs, quarter, width)
    out_cols = [lax.dynamic_slice_in_dim(gout, (tile ^ r) * part, part, 1) for r in range(4)]
    out_rows = scatter_tiles(out_cols)
    if direct:
        line = imgs // 2
        (g1, g2), out_cols = tie((g1, g2), out_cols)
        near1 = exchange_near(g1.reshape(line, 2, share, units))
        far2 = exchange_far(g2.reshape(line, 2, quarter, width))
    dctx, out_rows = tie(dctx, out_rows)
    out_rows = jnp.concatenate(own_order(out_rows, tile), axis=0)

    *mixed, gqkv, vecs = vec_call(
        functools.partial(attnback_kernel, cols=cols),
        [sds((toks, 3 * part))] * 4 + [sds((width, 3 * part)), sds((9, width), F32)],
        10,
        [
            pltpu.VMEM((part, total), F32),
            pltpu.VMEM((part, total), F32),
            pltpu.VMEM((total, 3 * part), BF),
        ],
        us=18,
    )(at_tile, patch_mask, dctx, qkv, lse, hid1, nrm1, w_own, bsum, vec2, fb2)

    vecs = vecs.reshape(9, imgs, share).transpose(1, 0, 2).reshape(imgs, 9 * share)
    count = 9 * share + quarter
    vec_height = -(-count // width)
    spare = jnp.zeros((imgs, vec_height * width - count), F32)
    vecs = jnp.concatenate([vecs, fb1.reshape(imgs, quarter), spare], axis=1).astype(BF)
    at_bucket = jnp.concatenate(
        [
            jnp.concatenate([gqkv, out_rows], axis=1).reshape(imgs, share, width),
            vecs.reshape(imgs, vec_height, width),
        ],
        axis=1,
    )
    if direct:
        near3 = exchange_near(at_bucket.reshape(line, 2, share + vec_height, width))
        near1, (at_bucket,) = tie(near1, (at_bucket,))
        mid1 = total_of(near1).astype(BF)
        far1 = exchange_far(mid1)
        (mixed, far2), (far1[0],) = tie((mixed, far2), (far1[0],))
    mixed_in = scatter_tiles(mixed)
    if direct:
        near2 = exchange_near(total_of(far2).astype(BF)[None])
        near3, (far1[0], mixed_in[0]) = tie(near3, (far1[0], mixed_in[0]))
        mid3 = total_of(near3).astype(BF)
        mixed_in[0], (mid3,) = tie(mixed_in[0], (mid3,))
        far3 = exchange_far(mid3)

    patches_grad = vec_call(
        input_kernel,
        sds((1, rows, cols, width)),
        8,
        [pltpu.VMEM((4, toks, 3 * part), BF), pltpu.VMEM((toks, width), BF)],
        us=5,
    )(at_tile, *mixed_in, qkv_weight, patches, rgrad, norm1_gain)

    if direct:
        fc2_sum = total_of(near2)[0].astype(BF)
        far1, (patches_grad,) = tie(far1, (patches_grad,))
        fc1_sum = total_of(far1).astype(BF)
    else:
        fc1_sum, fc2_sum, at_sum = (plain_sum(b) for b in (g1, g2, at_bucket))
    fc2_pieces, _ = gather_tiles(fc2_sum)
    fc1_pieces, _ = gather_tiles(fc1_sum)
    if direct:
        far3, (fc1_pieces[2], fc2_pieces[2], patches_grad) = tie(
            far3, (fc1_pieces[2], fc2_pieces[2], patches_grad)
        )
        at_sum = total_of(far3).astype(BF)
    fc1_grad, fc2_grad = vec_call(
        ffout_kernel,
        [sds((share, ff), F32), sds((4 * quarter, width), F32)],
        8,
        [pltpu.VMEM((4, max(share, quarter), width), F32)],
        us=3,
    )(at_tile, *fc1_pieces, *fc2_pieces)
    at_pieces, (fc1_grad, fc2_grad) = gather_tiles(at_sum, (fc1_grad, fc2_grad))
    qkv_grad, out_grad, *vec_sums, qv_sum, unit_sum = vec_call(
        attnout_kernel,
        [
            sds((share, 3 * width), F32),
            sds((share, width), F32),
            *[sds((share,), F32)] * 6,
            sds((share, 2), F32),
            sds((4 * quarter,), F32),
        ],
        4,
        [pltpu.VMEM((4, share + vec_height, width), F32)],
        us=3,
    )(at_tile, *at_pieces)
    return (
        layer_out,
        patches_grad,
        vec_sums[0],
        vec_sums[1],
        qkv_grad,
        qv_sum,
        out_grad,
        vec_sums[2],
        vec_sums[3],
        vec_sums[4],
        fc1_grad,
        unit_sum,
        fc2_grad,
        vec_sums[5],
    )


def solution(mesh):
    tiled = P("imgs", "rows", "cols", None)
    in_specs = (tiled, P("imgs", None, None)) + (P(),) * 12 + (tiled,)
    mat = P("imgs", None)
    vec = P("imgs")
    out_specs = (tiled, tiled, vec, vec, mat, mat, mat, vec, vec, vec, mat, vec, mat, vec)
    return jax.shard_map(layer, mesh=mesh, in_specs=in_specs, out_specs=out_specs, check_vma=False)
```

profile of v0, /device:TPU:0, one launch (start us, length us, event | category | flops | bytes accessed | tf_op | source)
XLA Modules:
  0.0 159.5 jit_solution(7231371833668967869)
XLA Ops:
  0.6 3.0 %collective-permute-start.2 = (bf16[1,15,15,768]{3,2,1,0:T(8,128)(2,1)}, bf16[1,15,15,768]{3,2,1,0:T(8,128)(2,1)S(1)}, u32[]{:S(2)}, u32[]{:S(2)}) collective-permute-start(bf16[1,15,15,768]{3,2,1,0:T(8,128)(2,1)} %x.3), channel_id=1, source_target_pairs={{0,16},{16,0},{1,17},{17,1},{2,18},{18,2},{3,19},{19,3},{4,20},{20... | collective-permute-start | bytes 1036808 | tf_op jit(solution)/shard_map/ppermute | solution.py:38
  3.7 4.5 %units.1 = (bf16[768,768]{1,0:T(8,128)(2,1)}, f32[1,768]{1,0:T(1,128)}) custom-call(s32[1]{0:T(128)} %bitcast.tile, bf16[768,3072]{1,0:T(8,128)(2,1)} %fc1.3, f32[1,3072]{1,0:T(1,128)} %bitcast.75), custom_call_target="tpu_custom_call" | custom-call | flops 4000000000 | bytes 4000000 | tf_op jit(solution)/shard_map/units/pallas_call | solution.py:522
  8.2 4.1 %heads.1 = (bf16[768,576]{1,0:T(8,128)(2,1)}, f32[1,576]{1,0:T(1,128)}) custom-call(s32[1]{0:T(128)} %bitcast.tile, bf16[768,2304]{1,0:T(8,128)(2,1)} %w.1, f32[2,768]{1,0:T(2,128)} %bitcast.77), custom_call_target="tpu_custom_call" | custom-call | flops 4000000000 | bytes 4000000 | tf_op jit(solution)/shard_map/heads/pallas_call | solution.py:506
  16.4 11.4 %shard_map.254 = (bf16[960,768]{1,0:T(8,128)(2,1)}, bf16[960,768]{1,0:T(8,128)(2,1)}, bf16[960,576]{1,0:T(8,128)(2,1)}, f32[960,128]{1,0:T(8,128)}, bf16[240,192...) custom-call(s32[1]{0:T(128)} %bitcast.tile, ...), custom_call_target="tpu_custom_call" | custom-call | flops 12999999488 | bytes 13000000 | tf_op jit(solution)/shard_map/pallas_call | solution.py:540
  29.7 2.4 %constant_dynamic-slice_fusion.5 = bf16[8,1,96,768]{3,2,1,0:T(8,128)(2,1)} fusion(bf16[8,4,96,768]{3,2,1,0:T(8,128)(2,1)} %bitcast.73, s32[]{:T(128)S(6)} %select_n.82), kind=kLoop, calls=%fused_computation.41 | loop fusion | bytes 2359300 | tf_op jit(solution)/shard_map/jit(dynamic_index_in_dim)/dynamic_slice | solution.py:556
  32.1 2.3 %collective-permute-done.5.c2 = bf16[240,192]{1,0:T(8,128)(2,1)S(1)} collective-permute-done((bf16[240,192]{1,0:T(8,128)(2,1)}, bf16[240,192]{1,0:T(8,128)(2,1)S(1)}, u32[]{:S(2)}, u32[]{:S(2)}) %collective-permute-start.5) | collective-permute-done | bytes 92192 | tf_op jit(solution)/shard_map/ppermute | solution.py:38
  36.4 3.1 %shard_map.255 = (f32[240,768]{1,0:T(8,128)}, bf16[240,768]{1,0:T(8,128)(2,1)}) custom-call(s32[1]{0:T(128)} %bitcast.tile, bf16[240,192]{1,0:T(8,128)(2,1)} %get-tuple-element.134.c0, bf16[240,192]{1,0:T(8,128)(2,1)} %copy-done.36, bf16[240,192]{1,0:T(8,128)(2,1)} %copy-done.37, bf16[240,192]{1,0:T(8,128)(2,1)} %copy-done.38, bf16[768,768]{1,0:T(8,128)(2,1)} %wo.3, ...), custom_call_target="tpu_custom_call" | custom-call | flops 3000000000 | bytes 3000000 | tf_op jit(solution)/shard_map/pallas_call | solution.py:562
  40.4 10.5 %mlp.1 = (bf16[1,15,15,768]{3,2,1,0:T(8,128)(2,1)}, bf16[240,768]{1,0:T(8,128)(2,1)}, f32[240,768]{1,0:T(8,128)}, f32[2,768]{1,0:T(2,128)}) custom-call(s32[1]{0:T(128)} %bitcast.tile, s32[1,30,30]{2,1,0:T(8,128)} %copy.59.mask, f32[240,768]{1,0:T(8,128)} %get-tuple-element.138.resid, bf16[240,768]{1,0:T(8,128)(2,1)} %get-tuple-element.139.hid.h0, ...), custom_call_target="tpu_custom_call" | custom-call | flops 11000000512 | bytes 11000000 | tf_op jit(solution)/shard_map/mlp/pallas_call | solution.py:576
  54.8 9.0 %shard_map.256 = (bf16[768,768]{1,0:T(8,128)(2,1)}, bf16[768,768]{1,0:T(8,128)(2,1)}, f32[1,768]{1,0:T(1,128)}, f32[1,768]{1,0:T(1,128)}) custom-call(s32[1]{0:T(128)} %bitcast.tile, s32[1,30,30]{2,1,0:T(8,128)} %copy.59.mask, bf16[240,768]{1,0:T(8,128)(2,1)} %get-tuple-element.139.hid.h0, bf16[240,768]{1,0:T(8,128)(2,1)} %copy-done.16, ...), custom_call_target="tpu_custom_call" | custom-call | flops 8999999488 | bytes 9000000 | tf_op jit(solution)/shard_map/pallas_call | solution.py:624
  66.5 3.6 %shard_map.257 = (bf16[960,192]{1,0:T(8,128)(2,1)}, bf16[192,768]{1,0:T(8,128)(2,1)}, f32[1,768]{1,0:T(1,128)}) custom-call(s32[1]{0:T(128)} %bitcast.tile, bf16[240,768]{1,0:T(8,128)(2,1)} %get-tuple-element.142.b0, bf16[240,768]{1,0:T(8,128)(2,1)} %copy-done.10, bf16[240,768]{1,0:T(8,128)(2,1)} %copy-done.9, bf16[240,768]{1,0:T(8,128)(2,1)} %copy-done.11, ...), custom_call_target="tpu_custom_call" | custom-call | flops 4000000000 | bytes 4000000 | tf_op jit(solution)/shard_map/pallas_call | solution.py:637
  73.4 1.6 collective-permute-start.22
  76.0 3.6 %collective-permute-start.19 = (bf16[2,96,768]{2,1,0:T(8,128)(2,1)}, bf16[2,96,768]{2,1,0:T(8,128)(2,1)S(1)}, u32[]{:S(2)}, u32[]{:S(2)}) collective-permute-start(bf16[2,96,768]{2,1,0:T(8,128)(2,1)} %get-tuple-element.286), channel_id=1, source_target_pairs={{0,6},{1,7},{2,4},{3,5},{4,2},{5,3},{6,0},{7,1},{8,14},{9,15},{10,... | collective-permute-start | bytes 884744 | tf_op jit(solution)/shard_map/ppermute | solution.py:95
  80.4 17.5 %shard_map.258 = (bf16[240,576]{1,0:T(8,128)(2,1)}, bf16[240,576]{1,0:T(8,128)(2,1)}, bf16[240,576]{1,0:T(8,128)(2,1)}, bf16[240,576]{1,0:T(8,128)(2,1)}, bf16[768,576]{1,0:T(8,128)(2,1)}, /*index=5*/f32[9,768]{1,0:T(8,128)}) custom-call(s32[1]{0:T(128)} %bitcast.tile, s32[1,30,30]{2,1,0:T(8,128)} %copy.59.mask, bf16[960,192]{1,0:T(8,128)(2,1)} %get-tuple-element.156.dctx, ...), custom_call_target="tpu_custom_call" | custom-call | flops 17999998976 | bytes 18000000 | tf_op jit(solution)/shard_map/pallas_call | solution.py:657
  101.6 3.7 %collective-permute-done.20 = bf16[2,96,768]{2,1,0:T(8,128)(2,1)} collective-permute-done((bf16[2,96,768]{2,1,0:T(8,128)(2,1)}, bf16[2,96,768]{2,1,0:T(8,128)(2,1)}, u32[]{:S(2)}, u32[]{:S(2)}) %collective-permute-start.20) | collective-permute-done | bytes 294944 | tf_op jit(solution)/shard_map/ppermute | solution.py:95
  109.0 8.3 %collective-permute-done.18 = bf16[4,98,768]{2,0,1:T(4,128)(2,1)S(1)} collective-permute-done((bf16[4,98,768]{2,0,1:T(4,128)(2,1)S(1)}, bf16[4,98,768]{2,0,1:T(4,128)(2,1)S(1)}, u32[]{:S(2)}, u32[]{:S(2)}) %collective-permute-start.18) | collective-permute-done | bytes 602144 | tf_op jit(solution)/shard_map/ppermute | solution.py:86
  117.3 3.5 %collective-permute-start.26 = (bf16[96,768]{1,0:T(8,128)(2,1)S(1)}, bf16[96,768]{1,0:T(8,128)(2,1)S(1)}, u32[]{:S(2)}, u32[]{:S(2)}) collective-permute-start(bf16[96,768]{1,0:T(8,128)(2,1)S(1)} %get-tuple-element.294), channel_id=1, source_target_pairs={{0,6},{1,7},{2,4},{3,5},{4,2},{5,3},{6,0},{7,1},{8,14},{9,15},{10,... | collective-permute-start | bytes 442376 | tf_op jit(solution)/shard_map/ppermute | solution.py:95
  121.3 1.8 %collective-permute-start.28 = (bf16[96,768]{1,0:T(8,128)(2,1)S(1)}, bf16[96,768]{1,0:T(8,128)(2,1)S(1)}, u32[]{:S(2)}, u32[]{:S(2)}) collective-permute-start(bf16[96,768]{1,0:T(8,128)(2,1)S(1)} %get-tuple-element.292), channel_id=1, source_target_pairs={{0,2},{1,3},{2,0},{3,1},{4,6},{5,7},{6,4},{7,5},{8,10},{9,11},{10,... | collective-permute-start | bytes 442376 | tf_op jit(solution)/shard_map/ppermute | solution.py:95
  123.1 2.5 %collective-permute-start.23 = (bf16[98,768]{1,0:T(8,128)(2,1)S(1)}, bf16[98,768]{1,0:T(8,128)(2,1)S(1)}, u32[]{:S(2)}, u32[]{:S(2)}) collective-permute-start(bf16[98,768]{1,0:T(8,128)(2,1)S(1)} %get-tuple-element.290), channel_id=1, source_target_pairs={{0,6},{1,7},{2,4},{3,5},{4,2},{5,3},{6,0},{7,1},{8,14},{9,15},{10,... | collective-permute-start | bytes 451592 | tf_op jit(solution)/shard_map/ppermute | solution.py:95
  126.3 4.9 %shard_map.259 = bf16[1,15,15,768]{3,2,1,0:T(8,128)(2,1)} custom-call(s32[1]{0:T(128)} %bitcast.tile, bf16[240,576]{1,0:T(8,128)(2,1)} %get-tuple-element.188.m0, bf16[240,576]{1,0:T(8,128)(2,1)} %copy-done.24, bf16[240,576]{1,0:T(8,128)(2,1)} %copy-done.25, bf16[240,576]{1,0:T(8,128)(2,1)} %copy-done.26, bf16[768,2304]{1,0:T(8,128)(2,1)} %w.1, ...), custom_call_target="tpu_custom_call" | custom-call | flops 5000000000 | bytes 5000000 | tf_op jit(solution)/shard_map/pallas_call | solution.py:695
  132.4 7.1 %collective-permute-done.27 = bf16[96,768]{1,0:T(8,128)(2,1)S(1)} collective-permute-done((bf16[96,768]{1,0:T(8,128)(2,1)S(1)}, bf16[96,768]{1,0:T(8,128)(2,1)S(1)}, u32[]{:S(2)}, u32[]{:S(2)}) %collective-permute-start.27) | collective-permute-done | bytes 147488 | tf_op jit(solution)/shard_map/ppermute | solution.py:95
  141.7 2.9 %collective-permute-done.34.b2 = bf16[96,768]{1,0:T(8,128)(2,1)S(1)} collective-permute-done((bf16[96,768]{1,0:T(8,128)(2,1)S(1)}, bf16[96,768]{1,0:T(8,128)(2,1)S(1)}, u32[]{:S(2)}, u32[]{:S(2)}) %collective-permute-start.34) | collective-permute-done | bytes 147488 | tf_op jit(solution)/shard_map/ppermute | solution.py:38
  144.7 1.6 collective-permute-done.32.a2
  149.8 3.4 %shard_map.260 = (f32[96,3072]{1,0:T(8,128)}, f32[384,768]{1,0:T(8,128)}) custom-call(s32[1]{0:T(128)} %bitcast.tile, bf16[96,768]{1,0:T(8,128)(2,1)} %copy-done.5, bf16[96,768]{1,0:T(8,128)(2,1)} %copy-done.33, bf16[96,768]{1,0:T(8,128)(2,1)} %copy-done.31, bf16[96,768]{1,0:T(8,128)(2,1)} %copy-done.35, bf16[96,768]{1,0:T(8,128)(2,1)} %copy-done.4, ...), custom_call_target="tpu_custom_call" | custom-call | flops 3000000000 | bytes 3000000 | tf_op jit(solution)/shard_map/pallas_call | solution.py:716
  155.5 2.6 %shard_map.261 = (f32[96,2304]{1,0:T(8,128)}, f32[96,768]{1,0:T(8,128)}, f32[96]{0:T(128)}, f32[96]{0:T(128)}, f32[96]{0:T(128)}, /*index=5*/f32[96]{0:T(128)}, ...) custom-call(s32[1]{0:T(128)} %bitcast.tile, bf16[98,768]{1,0:T(8,128)(2,1)} %copy-done.3, ...), custom_call_target="tpu_custom_call" | custom-call | flops 3000000000 | bytes 3000000 | tf_op jit(solution)/shard_map/pallas_call | solution.py:724
  (178 shorter events, 39.5 us)
Async XLA Ops:
  0.6 11.8 %collective-permute-start.2 = (bf16[1,15,15,768]{3,2,1,0:T(8,128)(2,1)}, bf16[1,15,15,768]{3,2,1,0:T(8,128)(2,1)S(1)}, u32[]{:S(2)}, u32[]{:S(2)}) collective-permute-start(bf16[1,15,15,768]{3,2,1,0:T(8,128)(2,1)} %x.3), channel_id=1, source_target_pairs={{0,16},{16,0},{1,17},{17,1},{2,18},{18,2},{3,19},{19,3},{4,20},{20... | collective-permute-start | bytes 1036808 | tf_op jit(solution)/shard_map/ppermute | solution.py:38
  3.7 11.2 %collective-permute-start.1 = (bf16[1,15,15,768]{3,2,1,0:T(8,128)(2,1)}, bf16[1,15,15,768]{3,2,1,0:T(8,128)(2,1)S(1)}, u32[]{:S(2)}, u32[]{:S(2)}) collective-permute-start(bf16[1,15,15,768]{3,2,1,0:T(8,128)(2,1)} %x.3), channel_id=1, source_target_pairs={{0,8},{8,0},{1,9},{9,1},{2,10},{10,2},{3,11},{11,3},{4,12},{12,4},... | collective-permute-start | bytes 1036808 | tf_op jit(solution)/shard_map/ppermute | solution.py:36
  12.9 14.8 %collective-permute-start = (bf16[1,15,15,768]{3,2,1,0:T(8,128)(2,1)S(1)}, bf16[1,15,15,768]{3,2,1,0:T(8,128)(2,1)S(1)}, u32[]{:S(2)}, u32[]{:S(2)}) collective-permute-start(bf16[1,15,15,768]{3,2,1,0:T(8,128)(2,1)S(1)} %copy-done.7), channel_id=1, source_target_pairs={{0,16},{16,0},{1,17},{17,1},{2,18},{18,2},{3,19},{19,3},{4,20},{20... | collective-permute-start | bytes 1036808 | tf_op jit(solution)/shard_map/ppermute | solution.py:38
  39.6 11.3 %collective-permute-start.7 = (bf16[240,768]{1,0:T(8,128)(2,1)}, bf16[240,768]{1,0:T(8,128)(2,1)S(1)}, u32[]{:S(2)}, u32[]{:S(2)}) collective-permute-start(bf16[240,768]{1,0:T(8,128)(2,1)} %get-tuple-element.139.hid.h0), channel_id=1, source_target_pairs={{0,16},{16,0},{1,17},{17,1},{2,18},{18,2},{3,19},{19,3},{4,20},{20... | collective-permute-start | bytes 1105928 | tf_op jit(solution)/shard_map/ppermute | solution.py:38
  40.3 13.5 %collective-permute-start.10 = (bf16[240,768]{1,0:T(8,128)(2,1)}, bf16[240,768]{1,0:T(8,128)(2,1)S(1)}, u32[]{:S(2)}, u32[]{:S(2)}) collective-permute-start(bf16[240,768]{1,0:T(8,128)(2,1)} %get-tuple-element.139.hid.h0), channel_id=1, source_target_pairs={{0,8},{8,0},{1,9},{9,1},{2,10},{10,2},{3,11},{11,3},{4,12},{12,4},... | collective-permute-start | bytes 1105928 | tf_op jit(solution)/shard_map/ppermute | solution.py:36
  51.9 11.9 %collective-permute-start.9 = (bf16[240,768]{1,0:T(8,128)(2,1)}, bf16[240,768]{1,0:T(8,128)(2,1)S(1)}, u32[]{:S(2)}, u32[]{:S(2)}) collective-permute-start(bf16[240,768]{1,0:T(8,128)(2,1)} %get-tuple-element.142.b0), channel_id=1, source_target_pairs={{0,16},{16,0},{1,17},{17,1},{2,18},{18,2},{3,19},{19,3},{4,20},{20... | collective-permute-start | bytes 1105928 | tf_op jit(solution)/shard_map/ppermute | solution.py:38
  53.3 11.8 %collective-permute-start.8 = (bf16[240,768]{1,0:T(8,128)(2,1)}, bf16[240,768]{1,0:T(8,128)(2,1)S(1)}, u32[]{:S(2)}, u32[]{:S(2)}) collective-permute-start(bf16[240,768]{1,0:T(8,128)(2,1)} %get-tuple-element.142.b0), channel_id=1, source_target_pairs={{0,8},{8,0},{1,9},{9,1},{2,10},{10,2},{3,11},{11,3},{4,12},{12,4},... | collective-permute-start | bytes 1105928 | tf_op jit(solution)/shard_map/ppermute | solution.py:36
  71.4 8.1 %collective-permute-start.15 = (bf16[192,192]{1,0:T(8,128)(2,1)S(1)}, bf16[192,192]{1,0:T(8,128)(2,1)}, u32[]{:S(2)}, u32[]{:S(2)}) collective-permute-start(bf16[192,192]{1,0:T(8,128)(2,1)S(1)} %get-tuple-element.302), channel_id=1, source_target_pairs={{0,8},{8,0},{1,9},{9,1},{2,10},{10,2},{3,11},{11,3},{4,12},{12,4},... | collective-permute-start | bytes 221192 | tf_op jit(solution)/shard_map/ppermute | solution.py:36
  71.6 7.9 %collective-permute-start.16 = (bf16[192,192]{1,0:T(8,128)(2,1)S(1)}, bf16[192,192]{1,0:T(8,128)(2,1)}, u32[]{:S(2)}, u32[]{:S(2)}) collective-permute-start(bf16[192,192]{1,0:T(8,128)(2,1)S(1)} %get-tuple-element.301), channel_id=1, source_target_pairs={{0,16},{16,0},{1,17},{17,1},{2,18},{18,2},{3,19},{19,3},{4,20},{20... | collective-permute-start | bytes 221192 | tf_op jit(solution)/shard_map/ppermute | solution.py:38
  73.4 27.9 %collective-permute-start.22 = (bf16[4,96,768]{2,1,0:T(8,128)(2,1)S(1)}, bf16[4,96,768]{2,1,0:T(8,128)(2,1)S(1)}, u32[]{:S(2)}, u32[]{:S(2)}) collective-permute-start(bf16[4,96,768]{2,1,0:T(8,128)(2,1)S(1)} %get-tuple-element.282), channel_id=1, source_target_pairs={{0,1},{1,0},{2,3},{3,2},{4,5},{5,4},{6,7},{7,6},{8,9},{9,8},{10,11... | collective-permute-start | bytes 1769480 | tf_op jit(solution)/shard_map/ppermute | solution.py:86
  76.0 25.6 %collective-permute-start.19 = (bf16[2,96,768]{2,1,0:T(8,128)(2,1)}, bf16[2,96,768]{2,1,0:T(8,128)(2,1)S(1)}, u32[]{:S(2)}, u32[]{:S(2)}) collective-permute-start(bf16[2,96,768]{2,1,0:T(8,128)(2,1)} %get-tuple-element.286), channel_id=1, source_target_pairs={{0,6},{1,7},{2,4},{3,5},{4,2},{5,3},{6,0},{7,1},{8,14},{9,15},{10,... | collective-permute-start | bytes 884744 | tf_op jit(solution)/shard_map/ppermute | solution.py:95
  79.6 25.8 %collective-permute-start.20 = (bf16[2,96,768]{2,1,0:T(8,128)(2,1)}, bf16[2,96,768]{2,1,0:T(8,128)(2,1)}, u32[]{:S(2)}, u32[]{:S(2)}) collective-permute-start(bf16[2,96,768]{2,1,0:T(8,128)(2,1)} %get-tuple-element.285), channel_id=1, source_target_pairs={{0,4},{1,5},{2,6},{3,7},{4,0},{5,1},{6,2},{7,3},{8,12},{9,13},{10,... | collective-permute-start | bytes 884744 | tf_op jit(solution)/shard_map/ppermute | solution.py:95
  79.6 25.8 %collective-permute-start.21 = (bf16[2,96,768]{2,1,0:T(8,128)(2,1)}, bf16[2,96,768]{2,1,0:T(8,128)(2,1)}, u32[]{:S(2)}, u32[]{:S(2)}) collective-permute-start(bf16[2,96,768]{2,1,0:T(8,128)(2,1)} %get-tuple-element.284), channel_id=1, source_target_pairs={{0,2},{1,3},{2,0},{3,1},{4,6},{5,7},{6,4},{7,5},{8,10},{9,11},{10,... | collective-permute-start | bytes 884744 | tf_op jit(solution)/shard_map/ppermute | solution.py:95
  100.8 16.5 %collective-permute-start.18 = (bf16[4,98,768]{2,0,1:T(4,128)(2,1)S(1)}, bf16[4,98,768]{2,0,1:T(4,128)(2,1)S(1)}, u32[]{:S(2)}, u32[]{:S(2)}) collective-permute-start(bf16[4,98,768]{2,0,1:T(4,128)(2,1)S(1)} %bitcast.71), channel_id=1, source_target_pairs={{0,1},{1,0},{2,3},{3,2},{4,5},{5,4},{6,7},{7,6},{8,9},{9,8},{10,11... | collective-permute-start | bytes 1806344 | tf_op jit(solution)/shard_map/ppermute | solution.py:86
  106.5 14.4 %collective-permute-start.33 = (bf16[1,96,768]{2,1,0:T(8,128)(2,1)S(1)}, bf16[1,96,768]{2,1,0:T(8,128)(2,1)S(1)}, u32[]{:S(2)}, u32[]{:S(2)}) collective-permute-start(bf16[1,96,768]{2,1,0:T(8,128)(2,1)S(1)} %constant_dynamic-slice_fusion), channel_id=1, source_target_pairs={{0,1},{1,0},{2,3},{3,2},{4,5},{5,4},{6,7},{7,6},{8,9},{9,8},{10,11... | collective-permute-start | bytes 442376 | tf_op jit(solution)/shard_map/ppermute | solution.py:86
  107.1 14.2 %collective-permute-start.29 = (bf16[240,576]{1,0:T(8,128)(2,1)S(1)}, bf16[240,576]{1,0:T(8,128)(2,1)S(1)}, u32[]{:S(2)}, u32[]{:S(2)}) collective-permute-start(bf16[240,576]{1,0:T(8,128)(2,1)S(1)} %copy-done.23), channel_id=1, source_target_pairs={{0,8},{8,0},{1,9},{9,1},{2,10},{10,2},{3,11},{11,3},{4,12},{12,4},... | collective-permute-start | bytes 829448 | tf_op jit(solution)/shard_map/ppermute | solution.py:36
  107.1 16.0 %collective-permute-start.30 = (bf16[240,576]{1,0:T(8,128)(2,1)S(1)}, bf16[240,576]{1,0:T(8,128)(2,1)S(1)}, u32[]{:S(2)}, u32[]{:S(2)}) collective-permute-start(bf16[240,576]{1,0:T(8,128)(2,1)S(1)} %copy-done.22), channel_id=1, source_target_pairs={{0,16},{16,0},{1,17},{17,1},{2,18},{18,2},{3,19},{19,3},{4,20},{20... | collective-permute-start | bytes 829448 | tf_op jit(solution)/shard_map/ppermute | solution.py:38
  108.5 17.1 %collective-permute-start.31 = (bf16[240,576]{1,0:T(8,128)(2,1)S(1)}, bf16[240,576]{1,0:T(8,128)(2,1)S(1)}, u32[]{:S(2)}, u32[]{:S(2)}) collective-permute-start(bf16[240,576]{1,0:T(8,128)(2,1)S(1)} %copy-done.21), channel_id=1, source_target_pairs={{0,24},{8,16},{16,8},{24,0},{1,25},{9,17},{17,9},{25,1},{2,26},{10... | collective-permute-start | bytes 829448 | tf_op jit(solution)/shard_map/ppermute | solution.py:39
  117.3 13.9 %collective-permute-start.26 = (bf16[96,768]{1,0:T(8,128)(2,1)S(1)}, bf16[96,768]{1,0:T(8,128)(2,1)S(1)}, u32[]{:S(2)}, u32[]{:S(2)}) collective-permute-start(bf16[96,768]{1,0:T(8,128)(2,1)S(1)} %get-tuple-element.294), channel_id=1, source_target_pairs={{0,6},{1,7},{2,4},{3,5},{4,2},{5,3},{6,0},{7,1},{8,14},{9,15},{10,... | collective-permute-start | bytes 442376 | tf_op jit(solution)/shard_map/ppermute | solution.py:95
  121.0 18.5 %collective-permute-start.27 = (bf16[96,768]{1,0:T(8,128)(2,1)S(1)}, bf16[96,768]{1,0:T(8,128)(2,1)S(1)}, u32[]{:S(2)}, u32[]{:S(2)}) collective-permute-start(bf16[96,768]{1,0:T(8,128)(2,1)S(1)} %get-tuple-element.293), channel_id=1, source_target_pairs={{0,4},{1,5},{2,6},{3,7},{4,0},{5,1},{6,2},{7,3},{8,12},{9,13},{10,... | collective-permute-start | bytes 442376 | tf_op jit(solution)/shard_map/ppermute | solution.py:95
  121.3 19.5 %collective-permute-start.28 = (bf16[96,768]{1,0:T(8,128)(2,1)S(1)}, bf16[96,768]{1,0:T(8,128)(2,1)S(1)}, u32[]{:S(2)}, u32[]{:S(2)}) collective-permute-start(bf16[96,768]{1,0:T(8,128)(2,1)S(1)} %get-tuple-element.292), channel_id=1, source_target_pairs={{0,2},{1,3},{2,0},{3,1},{4,6},{5,7},{6,4},{7,5},{8,10},{9,11},{10,... | collective-permute-start | bytes 442376 | tf_op jit(solution)/shard_map/ppermute | solution.py:95
  123.1 23.1 %collective-permute-start.23 = (bf16[98,768]{1,0:T(8,128)(2,1)S(1)}, bf16[98,768]{1,0:T(8,128)(2,1)S(1)}, u32[]{:S(2)}, u32[]{:S(2)}) collective-permute-start(bf16[98,768]{1,0:T(8,128)(2,1)S(1)} %get-tuple-element.290), channel_id=1, source_target_pairs={{0,6},{1,7},{2,4},{3,5},{4,2},{5,3},{6,0},{7,1},{8,14},{9,15},{10,... | collective-permute-start | bytes 451592 | tf_op jit(solution)/shard_map/ppermute | solution.py:95
  125.6 21.2 %collective-permute-start.24 = (bf16[98,768]{1,0:T(8,128)(2,1)S(1)}, bf16[98,768]{1,0:T(8,128)(2,1)S(1)}, u32[]{:S(2)}, u32[]{:S(2)}) collective-permute-start(bf16[98,768]{1,0:T(8,128)(2,1)S(1)} %get-tuple-element.289), channel_id=1, source_target_pairs={{0,4},{1,5},{2,6},{3,7},{4,0},{5,1},{6,2},{7,3},{8,12},{9,13},{10,... | collective-permute-start | bytes 451592 | tf_op jit(solution)/shard_map/ppermute | solution.py:95
  131.2 15.6 %collective-permute-start.25 = (bf16[98,768]{1,0:T(8,128)(2,1)S(1)}, bf16[98,768]{1,0:T(8,128)(2,1)S(1)}, u32[]{:S(2)}, u32[]{:S(2)}) collective-permute-start(bf16[98,768]{1,0:T(8,128)(2,1)S(1)} %get-tuple-element.288), channel_id=1, source_target_pairs={{0,2},{1,3},{2,0},{3,1},{4,6},{5,7},{6,4},{7,5},{8,10},{9,11},{10,... | collective-permute-start | bytes 451592 | tf_op jit(solution)/shard_map/ppermute | solution.py:95
  (57 other events, 224.0 us)
where the time goes:
time: 160 us
  Pallas kernels  74.6 us (47%)
  starting transfers between devices  35.2 us (22%)
  waiting for transfers between devices  29.8 us (19%)
  local copies, waits for them, and re-layouts  14.3 us (9%)
  other arithmetic  4.65 us (3%)
    pallas_call x1, Pallas kernels, layer(): vec_call(functools.partial(attnback_kernel, cols=cols), [sds((toks, 3 * p...  17.5 us
    ppermute x9, starting transfers between devices, exchange_far(): lax.ppermute(send, 'imgs', [(i, i ^ 2 * k) for i in range(count)])  13.6 us
    ppermute x10, starting transfers between devices, to_peer(): return lax.ppermute(value, 'rows', [(0, 1), (1, 0)])  13.1 us
    pallas_call x1, Pallas kernels, layer(): vec_call(attn_kernel, [sds((total, width)), sds((total, width)), sds((tot...  11.4 us
    ppermute x9, waiting for transfers between devices, exchange_far(): lax.ppermute(send, 'imgs', [(i, i ^ 2 * k) for i in range(count)])  10.8 us
    pallas_call x1, Pallas kernels, layer(): pl.pallas_call(mlp_kernel, grid=(chunks,), in_specs=[SMEM, whole(*patch_m...  10.5 us
    pallas_call x1, Pallas kernels, layer(): vec_call(ffgrad_kernel, [sds((width, units)), sds((units, width)), sds((1...  9.03 us
    unnamed x80, local copies, waits for them, and re-layouts  8.83 us
  transfers between devices with their start and end apart: 42, of which 12 were waited for; matrix products, arithmetic and copies ran while one was open for 6% of the time, Pallas kernels for 41%

commit v1 on v0

--- a/solution.py
+++ b/solution.py
@@ -106,11 +106,6 @@
 
 def plain_sum(parts):
     return lax.psum_scatter(parts, "imgs", scatter_dimension=0, tiled=False)
-
-
-def own_order(blocks, tile):
-    stacked = jnp.stack(blocks)
-    return [lax.dynamic_index_in_dim(stacked, tile ^ k, 0, keepdims=False) for k in range(4)]
 
 
 SMEM = pl.BlockSpec(memory_space=pltpu.SMEM)
@@ -348,11 +343,15 @@
     bsum,
     vec2,
     fb2,
+    o0,
+    o1,
+    o2,
+    o3,
     m0,
     m1,
     m2,
     m3,
-    gqkv,
+    grads,
     vecs,
     dk,
     dv,
@@ -393,7 +392,10 @@
     lax.fori_loop(0, 4, attend, 0)
     mix[:, part : 2 * part] = dk[...].T.astype(BF)
     mix[:, 2 * part :] = dv[...].T.astype(BF)
-    gqkv[...] = mm_tn(hid[...], mix[...]).astype(BF)
+    grads[:, : 3 * part] = mm_tn(hid[...], mix[...]).astype(BF)
+    for r, ref in enumerate((o0, o1, o2, o3)):
+        at = pl.multiple_of((tile[0] ^ r) * part, part)
+        grads[pl.ds(at, part), 3 * part :] = ref[...]
     for r, ref in enumerate((m0, m1, m2, m3)):
         ref[...] = mix[r * toks : (r + 1) * toks, :]
     col_sum = jnp.sum(mix[...].astype(F32), axis=0, keepdims=True)
@@ -428,23 +430,26 @@
     store_tile(out, (rgrad[...] + norm_back(n, normed, inv, vec_row(gain))).astype(BF))
 
 
-def ffout_kernel(tile, a0, a1, a2, a3, b0, b1, b2, b3, fc1, fc2, ps):
-    quarter = fc2.shape[0] // 4
-    for r, ref in enumerate((a0, a1, a2, a3)):
+def fc1out_kernel(tile, p0, p1, p2, p3, fc1, ps, *, quarter):
+    for r, ref in enumerate((p0, p1, p2, p3)):
         ps[r] = ref[...].astype(F32)
     for g in range(4):
         piece = ps[tile[0] ^ g]
         for i in range(fc1.shape[1] // (4 * quarter)):
             dst = (4 * i + g) * quarter
             fc1[:, dst : dst + quarter] = piece[:, i * quarter : (i + 1) * quarter]
-    for r, ref in enumerate((b0, b1, b2, b3)):
-        ps[r, :quarter, :] = ref[...].astype(F32)
+
+
+def fc2out_kernel(tile, p0, p1, p2, p3, fc2, ps):
+    quarter = fc2.shape[0] // 4
+    for r, ref in enumerate((p0, p1, p2, p3)):
+        ps[r] = ref[...].astype(F32)
     for g in range(4):
-        fc2[g * quarter : (g + 1) * quarter, :] = ps[tile[0] ^ g][:quarter]
+        fc2[g * quarter : (g + 1) * quarter, :] = ps[tile[0] ^ g]
 
 
 def attnout_kernel(
-    tile, p0, p1, p2, p3, gqkv, gout, v0, v1, v5, v6, v7, v8, qv, units, ps
+    tile, p0, p1, p2, p3, gqkv, gout, v0, v1, v2, v4, v5, v6, v7, v8, units, ps
 ):
     rows, width = gout.shape
     part = width // 4
@@ -463,10 +468,9 @@
         tail = jnp.concatenate([piece[rows + j : rows + j + 1] for j in range(height)], axis=1)
         total = tail if g == 0 else total + tail
         tails.append(tail[:, 9 * rows : 9 * rows + quarter])
-    for i, ref in ((0, v0), (1, v1), (5, v5), (6, v6), (7, v7), (8, v8)):
+    places = ((0, v0), (1, v1), (2, v2), (4, v4), (5, v5), (6, v6), (7, v7), (8, v8))
+    for i, ref in places:
         ref[...] = total[0, i * rows : (i + 1) * rows]
-    both = [total[:, i * rows : (i + 1) * rows] for i in (2, 4)]
-    qv[...] = jnp.concatenate(both, axis=0).T
     units[...] = jnp.concatenate(tails, axis=1)[0]
 
 
@@ -652,19 +656,18 @@
         near1 = exchange_near(g1.reshape(line, 2, share, units))
         far2 = exchange_far(g2.reshape(line, 2, quarter, width))
     dctx, out_rows = tie(dctx, out_rows)
-    out_rows = jnp.concatenate(own_order(out_rows, tile), axis=0)
-
-    *mixed, gqkv, vecs = vec_call(
+
+    *mixed, grads, vecs = vec_call(
         functools.partial(attnback_kernel, cols=cols),
-        [sds((toks, 3 * part))] * 4 + [sds((width, 3 * part)), sds((9, width), F32)],
-        10,
+        [sds((toks, 3 * part))] * 4 + [sds((width, width)), sds((9, width), F32)],
+        14,
         [
             pltpu.VMEM((part, total), F32),
             pltpu.VMEM((part, total), F32),
             pltpu.VMEM((total, 3 * part), BF),
         ],
         us=18,
-    )(at_tile, patch_mask, dctx, qkv, lse, hid1, nrm1, w_own, bsum, vec2, fb2)
+    )(at_tile, patch_mask, dctx, qkv, lse, hid1, nrm1, w_own, bsum, vec2, fb2, *out_rows)
 
     vecs = vecs.reshape(9, imgs, share).transpose(1, 0, 2).reshape(imgs, 9 * share)
     count = 9 * share + quarter
@@ -672,18 +675,14 @@
     spare = jnp.zeros((imgs, vec_height * width - count), F32)
     vecs = jnp.concatenate([vecs, fb1.reshape(imgs, quarter), spare], axis=1).astype(BF)
     at_bucket = jnp.concatenate(
-        [
-            jnp.concatenate([gqkv, out_rows], axis=1).reshape(imgs, share, width),
-            vecs.reshape(imgs, vec_height, width),
-        ],
-        axis=1,
+        [grads.reshape(imgs, share, width), vecs.reshape(imgs, vec_height, width)], axis=1
     )
     if direct:
         near3 = exchange_near(at_bucket.reshape(line, 2, share + vec_height, width))
         near1, (at_bucket,) = tie(near1, (at_bucket,))
         mid1 = total_of(near1).astype(BF)
         far1 = exchange_far(mid1)
-        (mixed, far2), (far1[0],) = tie((mixed, far2), (far1[0],))
+        far2, (far1[0],) = tie(far2, (far1[0],))
     mixed_in = scatter_tiles(mixed)
     if direct:
         near2 = exchange_near(total_of(far2).astype(BF)[None])
@@ -709,25 +708,29 @@
     fc2_pieces, _ = gather_tiles(fc2_sum)
     fc1_pieces, _ = gather_tiles(fc1_sum)
     if direct:
-        far3, (fc1_pieces[2], fc2_pieces[2], patches_grad) = tie(
-            far3, (fc1_pieces[2], fc2_pieces[2], patches_grad)
-        )
+        far3, (patches_grad, fc2_pieces[2]) = tie(far3, (patches_grad, fc2_pieces[2]))
         at_sum = total_of(far3).astype(BF)
-    fc1_grad, fc2_grad = vec_call(
-        ffout_kernel,
-        [sds((share, ff), F32), sds((4 * quarter, width), F32)],
-        8,
-        [pltpu.VMEM((4, max(share, quarter), width), F32)],
-        us=3,
-    )(at_tile, *fc1_pieces, *fc2_pieces)
+    fc2_grad = vec_call(
+        fc2out_kernel,
+        sds((4 * quarter, width), F32),
+        4,
+        [pltpu.VMEM((4, quarter, width), F32)],
+        us=2,
+    )(at_tile, *fc2_pieces)
+    fc1_grad = vec_call(
+        functools.partial(fc1out_kernel, quarter=quarter),
+        sds((share, ff), F32),
+        4,
+        [pltpu.VMEM((4, share, units), F32)],
+        us=2,
+    )(at_tile, *fc1_pieces)
     at_pieces, (fc1_grad, fc2_grad) = gather_tiles(at_sum, (fc1_grad, fc2_grad))
-    qkv_grad, out_grad, *vec_sums, qv_sum, unit_sum = vec_call(
+    qkv_grad, out_grad, *vec_sums, unit_sum = vec_call(
         attnout_kernel,
         [
             sds((share, 3 * width), F32),
             sds((share, width), F32),
-            *[sds((share,), F32)] * 6,
-            sds((share, 2), F32),
+            *[sds((share,), F32)] * 8,
             sds((4 * quarter,), F32),
         ],
         4,
@@ -740,15 +743,15 @@
         vec_sums[0],
         vec_sums[1],
         qkv_grad,
-        qv_sum,
+        jnp.stack([vec_sums[2], vec_sums[3]], axis=1),
         out_grad,
-        vec_sums[2],
-        vec_sums[3],
         vec_sums[4],
+        vec_sums[5],
+        vec_sums[6],
         fc1_grad,
         unit_sum,
         fc2_grad,
-        vec_sums[5],
+        vec_sums[7],
     )
 
 

time: 160 us -> 170 us (1.062)
  local copies, waits for them, and re-layouts: 14.3 us -> 22.1 us
  waiting for transfers between devices: 29.8 us -> 26.1 us
  Pallas kernels: 74.6 us -> 76.7 us
    ppermute x9, waiting for transfers between devices: 10.8 us -> 6.54 us  [exchange_far(): lax.ppermute(send, 'imgs', [(i, i ^ 2 * k) for i in range(count)])]
    reshape x3, local copies, waits for them, and re-layouts: 0.2 us -> 3.63 us  [layer(): vecs.reshape(9, imgs, share).transpose(1, 0, 2).reshape(imgs, 9 * share)]
    ppermute x3, waiting for transfers between devices: 8.31 us -> 10.4 us  [exchange_near(): lax.ppermute(send, 'imgs', [(i, i ^ 1) for i in range(count)])]
    pallas_call x1 -> x2, Pallas kernels: 3.39 us -> 5.03 us  [the longest x1 2.74 us: layer(): vec_call(functools.partial(fc1out_kernel, quarter=quarter), sds((share, f...]
    unnamed x80 -> x83, local copies, waits for them, and re-layouts: 8.83 us -> 9.65 us
  transfers between devices with their start and end apart: 42 -> 42, of which waited for: 12 -> 9; matrix products, arithmetic and copies ran while one was open for 6% -> 10% of each run, Pallas kernels for 41% -> 40%
where the time goes in v1:
time: 170 us; the launch traced here: 169 us
  Pallas kernels  76.7 us (45%)
  starting transfers between devices  36.9 us (22%)
  waiting for transfers between devices  26.1 us (15%)
  local copies, waits for them, and re-layouts  22.1 us (13%)
  other arithmetic  6.3 us (4%)
    pallas_call x1, Pallas kernels, layer(): vec_call(functools.partial(attnback_kernel, cols=cols), [sds((toks, 3 * p...  17.9 us
    ppermute x9, starting transfers between devices, exchange_far(): lax.ppermute(send, 'imgs', [(i, i ^ 2 * k) for i in range(count)])  14.2 us
    ppermute x10, starting transfers between devices, to_peer(): return lax.ppermute(value, 'rows', [(0, 1), (1, 0)])  13.2 us
    pallas_call x1, Pallas kernels, layer(): vec_call(attn_kernel, [sds((total, width)), sds((total, width)), sds((tot...  11.4 us
    pallas_call x1, Pallas kernels, layer(): pl.pallas_call(mlp_kernel, grid=(chunks,), in_specs=[SMEM, whole(*patch_m...  10.5 us
    ppermute x3, waiting for transfers between devices, exchange_near(): lax.ppermute(send, 'imgs', [(i, i ^ 1) for i in range(count)])  10.4 us
    unnamed x83, local copies, waits for them, and re-layouts  9.65 us
    pallas_call x1, Pallas kernels, layer(): vec_call(ffgrad_kernel, [sds((width, units)), sds((units, width)), sds((1...  9.03 us
  transfers between devices with their start and end apart: 42, of which 9 were waited for; matrix products, arithmetic and copies ran while one was open for 10% of the time, Pallas kernels for 40%

profile of v1, /device:TPU:0, one launch (start us, length us, event | category | flops | bytes accessed | tf_op | source)
XLA Modules:
  0.0 169.1 jit_solution(9372550580697754606)
XLA Ops:
  0.6 3.0 %collective-permute-start.2 = (bf16[1,15,15,768]{3,2,1,0:T(8,128)(2,1)}, bf16[1,15,15,768]{3,2,1,0:T(8,128)(2,1)S(1)}, u32[]{:S(2)}, u32[]{:S(2)}) collective-permute-start(bf16[1,15,15,768]{3,2,1,0:T(8,128)(2,1)} %x.3), channel_id=1, source_target_pairs={{0,16},{16,0},{1,17},{17,1},{2,18},{18,2},{3,19},{19,3},{4,20},{20... | collective-permute-start | bytes 1036808 | tf_op jit(solution)/shard_map/ppermute | solution.py:38
  3.7 4.5 %units.1 = (bf16[768,768]{1,0:T(8,128)(2,1)}, f32[1,768]{1,0:T(1,128)}) custom-call(s32[1]{0:T(128)} %bitcast.tile, bf16[768,3072]{1,0:T(8,128)(2,1)} %fc1.3, f32[1,3072]{1,0:T(1,128)} %bitcast.66), custom_call_target="tpu_custom_call" | custom-call | flops 4000000000 | bytes 4000000 | tf_op jit(solution)/shard_map/units/pallas_call | solution.py:526
  8.2 4.1 %heads.1 = (bf16[768,576]{1,0:T(8,128)(2,1)}, f32[1,576]{1,0:T(1,128)}) custom-call(s32[1]{0:T(128)} %bitcast.tile, bf16[768,2304]{1,0:T(8,128)(2,1)} %w.1, f32[2,768]{1,0:T(2,128)} %bitcast.68), custom_call_target="tpu_custom_call" | custom-call | flops 4000000000 | bytes 4000000 | tf_op jit(solution)/shard_map/heads/pallas_call | solution.py:510
  16.4 11.4 %shard_map.254 = (bf16[960,768]{1,0:T(8,128)(2,1)}, bf16[960,768]{1,0:T(8,128)(2,1)}, bf16[960,576]{1,0:T(8,128)(2,1)}, f32[960,128]{1,0:T(8,128)}, bf16[240,192...) custom-call(s32[1]{0:T(128)} %bitcast.tile, ...), custom_call_target="tpu_custom_call" | custom-call | flops 12999999488 | bytes 13000000 | tf_op jit(solution)/shard_map/pallas_call | solution.py:544
  29.7 2.4 %constant_dynamic-slice_fusion.5 = bf16[8,1,96,768]{3,2,1,0:T(8,128)(2,1)} fusion(bf16[8,4,96,768]{3,2,1,0:T(8,128)(2,1)} %bitcast.62, s32[]{:T(128)S(6)} %select_n.69), kind=kLoop, calls=%fused_computation.35 | loop fusion | bytes 2359300 | tf_op jit(solution)/shard_map/jit(dynamic_index_in_dim)/dynamic_slice | solution.py:560
  32.1 2.3 %collective-permute-done.5.c2 = bf16[240,192]{1,0:T(8,128)(2,1)S(1)} collective-permute-done((bf16[240,192]{1,0:T(8,128)(2,1)}, bf16[240,192]{1,0:T(8,128)(2,1)S(1)}, u32[]{:S(2)}, u32[]{:S(2)}) %collective-permute-start.5) | collective-permute-done | bytes 92192 | tf_op jit(solution)/shard_map/ppermute | solution.py:38
  36.5 3.1 %shard_map.255 = (f32[240,768]{1,0:T(8,128)}, bf16[240,768]{1,0:T(8,128)(2,1)}) custom-call(s32[1]{0:T(128)} %bitcast.tile, bf16[240,192]{1,0:T(8,128)(2,1)} %get-tuple-element.128.c0, bf16[240,192]{1,0:T(8,128)(2,1)} %copy-done.35, bf16[240,192]{1,0:T(8,128)(2,1)} %copy-done.36, bf16[240,192]{1,0:T(8,128)(2,1)} %copy-done.37, bf16[768,768]{1,0:T(8,128)(2,1)} %wo.3, ...), custom_call_target="tpu_custom_call" | custom-call | flops 3000000000 | bytes 3000000 | tf_op jit(solution)/shard_map/pallas_call | solution.py:566
  40.4 10.5 %mlp.1 = (bf16[1,15,15,768]{3,2,1,0:T(8,128)(2,1)}, bf16[240,768]{1,0:T(8,128)(2,1)}, f32[240,768]{1,0:T(8,128)}, f32[2,768]{1,0:T(2,128)}) custom-call(s32[1]{0:T(128)} %bitcast.tile, s32[1,30,30]{2,1,0:T(8,128)} %copy.56.mask, f32[240,768]{1,0:T(8,128)} %get-tuple-element.132.resid, bf16[240,768]{1,0:T(8,128)(2,1)} %get-tuple-element.133.hid.h0, ...), custom_call_target="tpu_custom_call" | custom-call | flops 11000000512 | bytes 11000000 | tf_op jit(solution)/shard_map/mlp/pallas_call | solution.py:580
  54.8 9.0 %shard_map.256 = (bf16[768,768]{1,0:T(8,128)(2,1)}, bf16[768,768]{1,0:T(8,128)(2,1)}, f32[1,768]{1,0:T(1,128)}, f32[1,768]{1,0:T(1,128)}) custom-call(s32[1]{0:T(128)} %bitcast.tile, s32[1,30,30]{2,1,0:T(8,128)} %copy.56.mask, bf16[240,768]{1,0:T(8,128)(2,1)} %get-tuple-element.133.hid.h0, bf16[240,768]{1,0:T(8,128)(2,1)} %copy-done.15, ...), custom_call_target="tpu_custom_call" | custom-call | flops 8999999488 | bytes 9000000 | tf_op jit(solution)/shard_map/pallas_call | solution.py:628
  67.1 3.6 %shard_map.257 = (bf16[960,192]{1,0:T(8,128)(2,1)}, bf16[192,768]{1,0:T(8,128)(2,1)}, f32[1,768]{1,0:T(1,128)}) custom-call(s32[1]{0:T(128)} %bitcast.tile, bf16[240,768]{1,0:T(8,128)(2,1)} %get-tuple-element.136.b0, bf16[240,768]{1,0:T(8,128)(2,1)} %copy-done.9, bf16[240,768]{1,0:T(8,128)(2,1)} %copy-done.8, bf16[240,768]{1,0:T(8,128)(2,1)} %copy-done.10, ...), custom_call_target="tpu_custom_call" | custom-call | flops 4000000000 | bytes 4000000 | tf_op jit(solution)/shard_map/pallas_call | solution.py:641
  70.7 1.9 %constant_dynamic-slice_fusion.1 = (bf16[192,192]{1,0:T(8,128)(2,1)S(1)}, bf16[192,192]{1,0:T(8,128)(2,1)S(1)}, bf16[192,192]{1,0:T(8,128)(2,1)S(1)}, bf16[192,192]{1,0:T(8,128)(2,1)}) fusion(bf16[192,768]{1,0:T(8,128)(2,1)} %get-tuple-element.149, s32[]{:T(128)S(6)} %select_n.73, s32[]{:T(128)S(6)} %select_n.72, s32[]{:T(128)S(6)} %select_n.71, s32[]{:T(128)S(6)} %select_n.70), kind=kLoop, calls=%fused_computation.31 | loop fusion | bytes 589840 | tf_op jit(solution)/shard_map/dynamic_slice | solution.py:651
  74.5 1.6 collective-permute-start.22
  76.2 3.7 %collective-permute-start.19 = (bf16[2,96,768]{2,1,0:T(8,128)(2,1)S(1)}, bf16[2,96,768]{2,1,0:T(8,128)(2,1)S(1)}, u32[]{:S(2)}, u32[]{:S(2)}) collective-permute-start(bf16[2,96,768]{2,1,0:T(8,128)(2,1)S(1)} %get-tuple-element.218), channel_id=1, source_target_pairs={{0,6},{1,7},{2,4},{3,5},{4,2},{5,3},{6,0},{7,1},{8,14},{9,15},{10,... | collective-permute-start | bytes 884744 | tf_op jit(solution)/shard_map/ppermute | solution.py:95
  81.3 17.9 %shard_map.258 = (bf16[240,576]{1,0:T(8,128)(2,1)}, bf16[240,576]{1,0:T(8,128)(2,1)}, bf16[240,576]{1,0:T(8,128)(2,1)}, bf16[240,576]{1,0:T(8,128)(2,1)}, bf16[768,768]{1,0:T(8,128)(2,1)}, /*index=5*/f32[9,768]{1,0:T(8,128)}) custom-call(s32[1]{0:T(128)} %bitcast.tile, s32[1,30,30]{2,1,0:T(8,128)} %copy.56.mask, bf16[960,192]{1,0:T(8,128)(2,1)} %get-tuple-element.150.dctx, ...), custom_call_target="tpu_custom_call" | custom-call | flops 17999998976 | bytes 18000000 | tf_op jit(solution)/shard_map/pallas_call | solution.py:660
  115.5 10.4 %collective-permute-done.18 = bf16[4,98,768]{2,0,1:T(4,128)(2,1)S(1)} collective-permute-done((bf16[4,98,768]{2,0,1:T(4,128)(2,1)S(1)}, bf16[4,98,768]{2,0,1:T(4,128)(2,1)S(1)}, u32[]{:S(2)}, u32[]{:S(2)}) %collective-permute-start.18) | collective-permute-done | bytes 602144 | tf_op jit(solution)/shard_map/ppermute | solution.py:86
  125.8 3.6 %collective-permute-start.26 = (bf16[96,768]{1,0:T(8,128)(2,1)S(1)}, bf16[96,768]{1,0:T(8,128)(2,1)S(1)}, u32[]{:S(2)}, u32[]{:S(2)}) collective-permute-start(bf16[96,768]{1,0:T(8,128)(2,1)S(1)} %get-tuple-element.226), channel_id=1, source_target_pairs={{0,6},{1,7},{2,4},{3,5},{4,2},{5,3},{6,0},{7,1},{8,14},{9,15},{10,... | collective-permute-start | bytes 442376 | tf_op jit(solution)/shard_map/ppermute | solution.py:95
  130.5 3.6 %collective-permute-start.23 = (bf16[98,768]{1,0:T(8,128)(2,1)S(1)}, bf16[98,768]{1,0:T(8,128)(2,1)S(1)}, u32[]{:S(2)}, u32[]{:S(2)}) collective-permute-start(bf16[98,768]{1,0:T(8,128)(2,1)S(1)} %get-tuple-element.222), channel_id=1, source_target_pairs={{0,6},{1,7},{2,4},{3,5},{4,2},{5,3},{6,0},{7,1},{8,14},{9,15},{10,... | collective-permute-start | bytes 451592 | tf_op jit(solution)/shard_map/ppermute | solution.py:95
  134.1 4.9 %shard_map.259 = bf16[1,15,15,768]{3,2,1,0:T(8,128)(2,1)} custom-call(s32[1]{0:T(128)} %bitcast.tile, bf16[240,576]{1,0:T(8,128)(2,1)} %get-tuple-element.178.m0, bf16[240,576]{1,0:T(8,128)(2,1)} %copy-done.23, bf16[240,576]{1,0:T(8,128)(2,1)} %copy-done.24, bf16[240,576]{1,0:T(8,128)(2,1)} %copy-done.25, bf16[768,2304]{1,0:T(8,128)(2,1)} %w.1, ...), custom_call_target="tpu_custom_call" | custom-call | flops 5000000000 | bytes 5000000 | tf_op jit(solution)/shard_map/pallas_call | solution.py:694
  139.1 1.8 %collective-permute-start.25 = (bf16[98,768]{1,0:T(8,128)(2,1)S(1)}, bf16[98,768]{1,0:T(8,128)(2,1)S(1)}, u32[]{:S(2)}, u32[]{:S(2)}) collective-permute-start(bf16[98,768]{1,0:T(8,128)(2,1)S(1)} %get-tuple-element.220), channel_id=1, source_target_pairs={{0,2},{1,3},{2,0},{3,1},{4,6},{5,7},{6,4},{7,5},{8,10},{9,11},{10,... | collective-permute-start | bytes 451592 | tf_op jit(solution)/shard_map/ppermute | solution.py:95
  140.8 6.5 %collective-permute-done.27 = bf16[96,768]{1,0:T(8,128)(2,1)S(1)} collective-permute-done((bf16[96,768]{1,0:T(8,128)(2,1)S(1)}, bf16[96,768]{1,0:T(8,128)(2,1)S(1)}, u32[]{:S(2)}, u32[]{:S(2)}) %collective-permute-start.27) | collective-permute-done | bytes 147488 | tf_op jit(solution)/shard_map/ppermute | solution.py:95
  149.5 3.0 %collective-permute-done.33.p2 = bf16[96,768]{1,0:T(8,128)(2,1)S(1)} collective-permute-done((bf16[96,768]{1,0:T(8,128)(2,1)S(1)}, bf16[96,768]{1,0:T(8,128)(2,1)S(1)}, u32[]{:S(2)}, u32[]{:S(2)}) %collective-permute-start.33) | collective-permute-done | bytes 147488 | tf_op jit(solution)/shard_map/ppermute | solution.py:38
  156.9 2.7 %shard_map.260 = f32[96,3072]{1,0:T(8,128)} custom-call(s32[1]{0:T(128)} %bitcast.tile, bf16[96,768]{1,0:T(8,128)(2,1)} %copy-done.4, bf16[96,768]{1,0:T(8,128)(2,1)} %copy-done.33, bf16[96,768]{1,0:T(8,128)(2,1)} %copy-done.31, bf16[96,768]{1,0:T(8,128)(2,1)} %copy-done.34), custom_call_target="tpu_custom_call" | custom-call | flops 2000000000 | bytes 2000000 | tf_op jit(solution)/shard_map/pallas_call | solution.py:720
  161.0 2.3 %shard_map.261 = f32[384,768]{1,0:T(8,128)} custom-call(s32[1]{0:T(128)} %bitcast.tile, bf16[96,768]{1,0:T(8,128)(2,1)} %copy-done.3, bf16[96,768]{1,0:T(8,128)(2,1)} %copy-done.30, bf16[96,768]{1,0:T(8,128)(2,1)} %copy-done.29, bf16[96,768]{1,0:T(8,128)(2,1)} %copy-done.32), custom_call_target="tpu_custom_call" | custom-call | flops 2000000000 | bytes 2000000 | tf_op jit(solution)/shard_map/pallas_call | solution.py:713
  165.4 2.5 %shard_map.262 = (f32[96,2304]{1,0:T(8,128)}, f32[96,768]{1,0:T(8,128)}, f32[96]{0:T(128)}, f32[96]{0:T(128)}, f32[96]{0:T(128)}, /*index=5*/f32[96]{0:T(128)}, ...) custom-call(s32[1]{0:T(128)} %bitcast.tile, bf16[98,768]{1,0:T(8,128)(2,1)} %copy-done.2, ...), custom_call_target="tpu_custom_call" | custom-call | flops 3000000000 | bytes 3000000 | tf_op jit(solution)/shard_map/pallas_call | solution.py:728
  (180 shorter events, 47.8 us)
Async XLA Ops:
  0.6 11.8 %collective-permute-start.2 = (bf16[1,15,15,768]{3,2,1,0:T(8,128)(2,1)}, bf16[1,15,15,768]{3,2,1,0:T(8,128)(2,1)S(1)}, u32[]{:S(2)}, u32[]{:S(2)}) collective-permute-start(bf16[1,15,15,768]{3,2,1,0:T(8,128)(2,1)} %x.3), channel_id=1, source_target_pairs={{0,16},{16,0},{1,17},{17,1},{2,18},{18,2},{3,19},{19,3},{4,20},{20... | collective-permute-start | bytes 1036808 | tf_op jit(solution)/shard_map/ppermute | solution.py:38
  3.7 11.2 %collective-permute-start.1 = (bf16[1,15,15,768]{3,2,1,0:T(8,128)(2,1)}, bf16[1,15,15,768]{3,2,1,0:T(8,128)(2,1)S(1)}, u32[]{:S(2)}, u32[]{:S(2)}) collective-permute-start(bf16[1,15,15,768]{3,2,1,0:T(8,128)(2,1)} %x.3), channel_id=1, source_target_pairs={{0,8},{8,0},{1,9},{9,1},{2,10},{10,2},{3,11},{11,3},{4,12},{12,4},... | collective-permute-start | bytes 1036808 | tf_op jit(solution)/shard_map/ppermute | solution.py:36
  12.9 14.8 %collective-permute-start = (bf16[1,15,15,768]{3,2,1,0:T(8,128)(2,1)S(1)}, bf16[1,15,15,768]{3,2,1,0:T(8,128)(2,1)S(1)}, u32[]{:S(2)}, u32[]{:S(2)}) collective-permute-start(bf16[1,15,15,768]{3,2,1,0:T(8,128)(2,1)S(1)} %copy-done.6), channel_id=1, source_target_pairs={{0,16},{16,0},{1,17},{17,1},{2,18},{18,2},{3,19},{19,3},{4,20},{20... | collective-permute-start | bytes 1036808 | tf_op jit(solution)/shard_map/ppermute | solution.py:38
  39.6 11.3 %collective-permute-start.7 = (bf16[240,768]{1,0:T(8,128)(2,1)}, bf16[240,768]{1,0:T(8,128)(2,1)S(1)}, u32[]{:S(2)}, u32[]{:S(2)}) collective-permute-start(bf16[240,768]{1,0:T(8,128)(2,1)} %get-tuple-element.133.hid.h0), channel_id=1, source_target_pairs={{0,16},{16,0},{1,17},{17,1},{2,18},{18,2},{3,19},{19,3},{4,20},{20... | collective-permute-start | bytes 1105928 | tf_op jit(solution)/shard_map/ppermute | solution.py:38
  40.3 13.5 %collective-permute-start.10 = (bf16[240,768]{1,0:T(8,128)(2,1)}, bf16[240,768]{1,0:T(8,128)(2,1)S(1)}, u32[]{:S(2)}, u32[]{:S(2)}) collective-permute-start(bf16[240,768]{1,0:T(8,128)(2,1)} %get-tuple-element.133.hid.h0), channel_id=1, source_target_pairs={{0,8},{8,0},{1,9},{9,1},{2,10},{10,2},{3,11},{11,3},{4,12},{12,4},... | collective-permute-start | bytes 1105928 | tf_op jit(solution)/shard_map/ppermute | solution.py:36
  51.9 11.9 %collective-permute-start.9 = (bf16[240,768]{1,0:T(8,128)(2,1)}, bf16[240,768]{1,0:T(8,128)(2,1)S(1)}, u32[]{:S(2)}, u32[]{:S(2)}) collective-permute-start(bf16[240,768]{1,0:T(8,128)(2,1)} %get-tuple-element.136.b0), channel_id=1, source_target_pairs={{0,16},{16,0},{1,17},{17,1},{2,18},{18,2},{3,19},{19,3},{4,20},{20... | collective-permute-start | bytes 1105928 | tf_op jit(solution)/shard_map/ppermute | solution.py:38
  53.3 12.4 %collective-permute-start.8 = (bf16[240,768]{1,0:T(8,128)(2,1)}, bf16[240,768]{1,0:T(8,128)(2,1)S(1)}, u32[]{:S(2)}, u32[]{:S(2)}) collective-permute-start(bf16[240,768]{1,0:T(8,128)(2,1)} %get-tuple-element.136.b0), channel_id=1, source_target_pairs={{0,8},{8,0},{1,9},{9,1},{2,10},{10,2},{3,11},{11,3},{4,12},{12,4},... | collective-permute-start | bytes 1105928 | tf_op jit(solution)/shard_map/ppermute | solution.py:36
  74.5 35.6 %collective-permute-start.22 = (bf16[4,96,768]{2,1,0:T(8,128)(2,1)S(1)}, bf16[4,96,768]{2,1,0:T(8,128)(2,1)S(1)}, u32[]{:S(2)}, u32[]{:S(2)}) collective-permute-start(bf16[4,96,768]{2,1,0:T(8,128)(2,1)S(1)} %get-tuple-element.214), channel_id=1, source_target_pairs={{0,1},{1,0},{2,3},{3,2},{4,5},{5,4},{6,7},{7,6},{8,9},{9,8},{10,11... | collective-permute-start | bytes 1769480 | tf_op jit(solution)/shard_map/ppermute | solution.py:86
  76.2 34.2 %collective-permute-start.19 = (bf16[2,96,768]{2,1,0:T(8,128)(2,1)S(1)}, bf16[2,96,768]{2,1,0:T(8,128)(2,1)S(1)}, u32[]{:S(2)}, u32[]{:S(2)}) collective-permute-start(bf16[2,96,768]{2,1,0:T(8,128)(2,1)S(1)} %get-tuple-element.218), channel_id=1, source_target_pairs={{0,6},{1,7},{2,4},{3,5},{4,2},{5,3},{6,0},{7,1},{8,14},{9,15},{10,... | collective-permute-start | bytes 884744 | tf_op jit(solution)/shard_map/ppermute | solution.py:95
  79.9 32.6 %collective-permute-start.20 = (bf16[2,96,768]{2,1,0:T(8,128)(2,1)S(1)}, bf16[2,96,768]{2,1,0:T(8,128)(2,1)S(1)}, u32[]{:S(2)}, u32[]{:S(2)}) collective-permute-start(bf16[2,96,768]{2,1,0:T(8,128)(2,1)S(1)} %get-tuple-element.217), channel_id=1, source_target_pairs={{0,4},{1,5},{2,6},{3,7},{4,0},{5,1},{6,2},{7,3},{8,12},{9,13},{10,... | collective-permute-start | bytes 884744 | tf_op jit(solution)/shard_map/ppermute | solution.py:95
  79.9 33.1 %collective-permute-start.21 = (bf16[2,96,768]{2,1,0:T(8,128)(2,1)S(1)}, bf16[2,96,768]{2,1,0:T(8,128)(2,1)}, u32[]{:S(2)}, u32[]{:S(2)}) collective-permute-start(bf16[2,96,768]{2,1,0:T(8,128)(2,1)S(1)} %get-tuple-element.216), channel_id=1, source_target_pairs={{0,2},{1,3},{2,0},{3,1},{4,6},{5,7},{6,4},{7,5},{8,10},{9,11},{10,... | collective-permute-start | bytes 884744 | tf_op jit(solution)/shard_map/ppermute | solution.py:95
  109.3 16.5 %collective-permute-start.18 = (bf16[4,98,768]{2,0,1:T(4,128)(2,1)S(1)}, bf16[4,98,768]{2,0,1:T(4,128)(2,1)S(1)}, u32[]{:S(2)}, u32[]{:S(2)}) collective-permute-start(bf16[4,98,768]{2,0,1:T(4,128)(2,1)S(1)} %bitcast.61), channel_id=1, source_target_pairs={{0,1},{1,0},{2,3},{3,2},{4,5},{5,4},{6,7},{7,6},{8,9},{9,8},{10,11... | collective-permute-start | bytes 1806344 | tf_op jit(solution)/shard_map/ppermute | solution.py:86
  110.2 19.4 %collective-permute-start.29 = (bf16[240,576]{1,0:T(8,128)(2,1)S(1)}, bf16[240,576]{1,0:T(8,128)(2,1)S(1)}, u32[]{:S(2)}, u32[]{:S(2)}) collective-permute-start(bf16[240,576]{1,0:T(8,128)(2,1)S(1)} %copy-done.22), channel_id=1, source_target_pairs={{0,8},{8,0},{1,9},{9,1},{2,10},{10,2},{3,11},{11,3},{4,12},{12,4},... | collective-permute-start | bytes 829448 | tf_op jit(solution)/shard_map/ppermute | solution.py:36
  111.2 18.5 %collective-permute-start.30 = (bf16[240,576]{1,0:T(8,128)(2,1)S(1)}, bf16[240,576]{1,0:T(8,128)(2,1)S(1)}, u32[]{:S(2)}, u32[]{:S(2)}) collective-permute-start(bf16[240,576]{1,0:T(8,128)(2,1)S(1)} %copy-done.21), channel_id=1, source_target_pairs={{0,16},{16,0},{1,17},{17,1},{2,18},{18,2},{3,19},{19,3},{4,20},{20... | collective-permute-start | bytes 829448 | tf_op jit(solution)/shard_map/ppermute | solution.py:38
  112.5 18.0 %collective-permute-start.31 = (bf16[240,576]{1,0:T(8,128)(2,1)S(1)}, bf16[240,576]{1,0:T(8,128)(2,1)S(1)}, u32[]{:S(2)}, u32[]{:S(2)}) collective-permute-start(bf16[240,576]{1,0:T(8,128)(2,1)S(1)} %copy-done.20), channel_id=1, source_target_pairs={{0,24},{8,16},{16,8},{24,0},{1,25},{9,17},{17,9},{25,1},{2,26},{10... | collective-permute-start | bytes 829448 | tf_op jit(solution)/shard_map/ppermute | solution.py:39
  114.2 24.8 %collective-permute-start.32 = (bf16[1,96,768]{2,1,0:T(8,128)(2,1)S(1)}, bf16[1,96,768]{2,1,0:T(8,128)(2,1)S(1)}, u32[]{:S(2)}, u32[]{:S(2)}) collective-permute-start(bf16[1,96,768]{2,1,0:T(8,128)(2,1)S(1)} %constant_dynamic-slice_fusion), channel_id=1, source_target_pairs={{0,1},{1,0},{2,3},{3,2},{4,5},{5,4},{6,7},{7,6},{8,9},{9,8},{10,11... | collective-permute-start | bytes 442376 | tf_op jit(solution)/shard_map/ppermute | solution.py:86
  125.8 13.2 %collective-permute-start.26 = (bf16[96,768]{1,0:T(8,128)(2,1)S(1)}, bf16[96,768]{1,0:T(8,128)(2,1)S(1)}, u32[]{:S(2)}, u32[]{:S(2)}) collective-permute-start(bf16[96,768]{1,0:T(8,128)(2,1)S(1)} %get-tuple-element.226), channel_id=1, source_target_pairs={{0,6},{1,7},{2,4},{3,5},{4,2},{5,3},{6,0},{7,1},{8,14},{9,15},{10,... | collective-permute-start | bytes 442376 | tf_op jit(solution)/shard_map/ppermute | solution.py:95
  129.6 17.7 %collective-permute-start.27 = (bf16[96,768]{1,0:T(8,128)(2,1)S(1)}, bf16[96,768]{1,0:T(8,128)(2,1)S(1)}, u32[]{:S(2)}, u32[]{:S(2)}) collective-permute-start(bf16[96,768]{1,0:T(8,128)(2,1)S(1)} %get-tuple-element.225), channel_id=1, source_target_pairs={{0,4},{1,5},{2,6},{3,7},{4,0},{5,1},{6,2},{7,3},{8,12},{9,13},{10,... | collective-permute-start | bytes 442376 | tf_op jit(solution)/shard_map/ppermute | solution.py:95
  129.7 19.0 %collective-permute-start.28 = (bf16[96,768]{1,0:T(8,128)(2,1)S(1)}, bf16[96,768]{1,0:T(8,128)(2,1)S(1)}, u32[]{:S(2)}, u32[]{:S(2)}) collective-permute-start(bf16[96,768]{1,0:T(8,128)(2,1)S(1)} %get-tuple-element.224), channel_id=1, source_target_pairs={{0,2},{1,3},{2,0},{3,1},{4,6},{5,7},{6,4},{7,5},{8,10},{9,11},{10,... | collective-permute-start | bytes 442376 | tf_op jit(solution)/shard_map/ppermute | solution.py:95
  130.5 22.0 %collective-permute-start.23 = (bf16[98,768]{1,0:T(8,128)(2,1)S(1)}, bf16[98,768]{1,0:T(8,128)(2,1)S(1)}, u32[]{:S(2)}, u32[]{:S(2)}) collective-permute-start(bf16[98,768]{1,0:T(8,128)(2,1)S(1)} %get-tuple-element.222), channel_id=1, source_target_pairs={{0,6},{1,7},{2,4},{3,5},{4,2},{5,3},{6,0},{7,1},{8,14},{9,15},{10,... | collective-permute-start | bytes 451592 | tf_op jit(solution)/shard_map/ppermute | solution.py:95
  139.0 14.0 %collective-permute-start.24 = (bf16[98,768]{1,0:T(8,128)(2,1)S(1)}, bf16[98,768]{1,0:T(8,128)(2,1)S(1)}, u32[]{:S(2)}, u32[]{:S(2)}) collective-permute-start(bf16[98,768]{1,0:T(8,128)(2,1)S(1)} %get-tuple-element.221), channel_id=1, source_target_pairs={{0,4},{1,5},{2,6},{3,7},{4,0},{5,1},{6,2},{7,3},{8,12},{9,13},{10,... | collective-permute-start | bytes 451592 | tf_op jit(solution)/shard_map/ppermute | solution.py:95
  139.1 14.0 %collective-permute-start.25 = (bf16[98,768]{1,0:T(8,128)(2,1)S(1)}, bf16[98,768]{1,0:T(8,128)(2,1)S(1)}, u32[]{:S(2)}, u32[]{:S(2)}) collective-permute-start(bf16[98,768]{1,0:T(8,128)(2,1)S(1)} %get-tuple-element.220), channel_id=1, source_target_pairs={{0,2},{1,3},{2,0},{3,1},{4,6},{5,7},{6,4},{7,5},{8,10},{9,11},{10,... | collective-permute-start | bytes 451592 | tf_op jit(solution)/shard_map/ppermute | solution.py:95
  154.2 9.1 %collective-permute-start.35 = (bf16[98,768]{1,0:T(8,128)(2,1)S(1)}, bf16[98,768]{1,0:T(8,128)(2,1)S(1)}, u32[]{:S(2)}, u32[]{:S(2)}) collective-permute-start(bf16[98,768]{1,0:T(8,128)(2,1)S(1)} %add_convert_fusion.3.p0), channel_id=1, source_target_pairs={{0,16},{16,0},{1,17},{17,1},{2,18},{18,2},{3,19},{19,3},{4,20},{20... | collective-permute-start | bytes 451592 | tf_op jit(solution)/shard_map/ppermute | solution.py:38
  155.6 7.9 %collective-permute-start.34 = (bf16[98,768]{1,0:T(8,128)(2,1)S(1)}, bf16[98,768]{1,0:T(8,128)(2,1)S(1)}, u32[]{:S(2)}, u32[]{:S(2)}) collective-permute-start(bf16[98,768]{1,0:T(8,128)(2,1)S(1)} %add_convert_fusion.3.p0), channel_id=1, source_target_pairs={{0,8},{8,0},{1,9},{9,1},{2,10},{10,2},{3,11},{11,3},{4,12},{12,4},... | collective-permute-start | bytes 451592 | tf_op jit(solution)/shard_map/ppermute | solution.py:36
  (59 other events, 225.0 us)

commit v2 on v1

--- a/solution.py
+++ b/solution.py
@@ -342,6 +342,7 @@
     w,
     bsum,
     vec2,
+    fb1,
     fb2,
     o0,
     o1,
@@ -352,10 +353,11 @@
     m2,
     m3,
     grads,
-    vecs,
+    rows_out,
     dk,
     dv,
     mix,
+    vecs,
     *,
     cols,
 ):
@@ -414,6 +416,16 @@
     vecs[5:6, :] = bsum[...] * lone
     vecs[6:8, :] = vec2[...]
     vecs[8:9, :] = fb2[...] * lone
+    imgs, height, width = rows_out.shape
+    share = width // imgs
+    quarter = fb1.shape[1] // imgs
+    spare = jnp.zeros((1, height * width - 9 * share - quarter), F32)
+    for i in range(imgs):
+        pieces = [vecs[j : j + 1, i * share : (i + 1) * share] for j in range(9)]
+        pieces += [fb1[:, i * quarter : (i + 1) * quarter], spare]
+        line = jnp.concatenate(pieces, axis=1).astype(BF)
+        for j in range(height):
+            rows_out[i, j : j + 1, :] = line[:, j * width : (j + 1) * width]
 
 
 def input_kernel(tile, m0, m1, m2, m3, w, x, rgrad, gain, out, ms, xs):
@@ -657,25 +669,23 @@
         far2 = exchange_far(g2.reshape(line, 2, quarter, width))
     dctx, out_rows = tie(dctx, out_rows)
 
+    count = 9 * share + quarter
+    vec_height = -(-count // width)
     *mixed, grads, vecs = vec_call(
         functools.partial(attnback_kernel, cols=cols),
-        [sds((toks, 3 * part))] * 4 + [sds((width, width)), sds((9, width), F32)],
-        14,
+        [sds((toks, 3 * part))] * 4 + [sds((width, width)), sds((imgs, vec_height, width))],
+        15,
         [
             pltpu.VMEM((part, total), F32),
             pltpu.VMEM((part, total), F32),
             pltpu.VMEM((total, 3 * part), BF),
+            pltpu.VMEM((9, width), F32),
         ],
         us=18,
-    )(at_tile, patch_mask, dctx, qkv, lse, hid1, nrm1, w_own, bsum, vec2, fb2, *out_rows)
-
-    vecs = vecs.reshape(9, imgs, share).transpose(1, 0, 2).reshape(imgs, 9 * share)
-    count = 9 * share + quarter
-    vec_height = -(-count // width)
-    spare = jnp.zeros((imgs, vec_height * width - count), F32)
-    vecs = jnp.concatenate([vecs, fb1.reshape(imgs, quarter), spare], axis=1).astype(BF)
+    )(at_tile, patch_mask, dctx, qkv, lse, hid1, nrm1, w_own, bsum, vec2, fb1, fb2, *out_rows)
+
     at_bucket = jnp.concatenate(
-        [grads.reshape(imgs, share, width), vecs.reshape(imgs, vec_height, width)], axis=1
+        [grads.reshape(imgs, share, width), vecs], axis=1
     )
     if direct:
         near3 = exchange_near(at_bucket.reshape(line, 2, share + vec_height, width))

time: 170 us -> 161 us (0.947)
  local copies, waits for them, and re-layouts: 22.1 us -> 13.7 us
  other arithmetic: 6.3 us -> 4.19 us
    reshape x4 -> x0, local copies, waits for them, and re-layouts: 4.3 us -> none  [the longest x3 3.63 us: layer(): vecs.reshape(9, imgs, share).transpose(1, 0, 2).reshape(imgs, 9 * share)]
    another operation x2 -> x0, other arithmetic: 2.11 us -> none
  transfers between devices with their start and end apart: 42 -> 42, of which waited for: 9 -> 11; matrix products, arithmetic and copies ran while one was open for 10% -> 4% of each run, Pallas kernels for 40% -> 42%
where the time goes in v2:
time: 161 us
  Pallas kernels  77.1 us (48%)
  starting transfers between devices  37.8 us (23%)
  waiting for transfers between devices  27 us (17%)
  local copies, waits for them, and re-layouts  13.7 us (9%)
  other arithmetic  4.19 us (3%)
    pallas_call x1, Pallas kernels, layer(): vec_call(functools.partial(attnback_kernel, cols=cols), [sds((toks, 3 * p...  18.3 us
    ppermute x9, starting transfers between devices, exchange_far(): lax.ppermute(send, 'imgs', [(i, i ^ 2 * k) for i in range(count)])  15.8 us
    ppermute x10, starting transfers between devices, to_peer(): return lax.ppermute(value, 'rows', [(0, 1), (1, 0)])  13.3 us
    pallas_call x1, Pallas kernels, layer(): vec_call(attn_kernel, [sds((total, width)), sds((total, width)), sds((tot...  11.4 us
    pallas_call x1, Pallas kernels, layer(): pl.pallas_call(mlp_kernel, grid=(chunks,), in_specs=[SMEM, whole(*patch_m...  10.5 us
    ppermute x3, waiting for transfers between devices, exchange_near(): lax.ppermute(send, 'imgs', [(i, i ^ 1) for i in range(count)])  10.2 us
    pallas_call x1, Pallas kernels, layer(): vec_call(ffgrad_kernel, [sds((width, units)), sds((units, width)), sds((1...  9.02 us
    unnamed x83, local copies, waits for them, and re-layouts  8.94 us
  transfers between devices with their start and end apart: 42, of which 11 were waited for; matrix products, arithmetic and copies ran while one was open for 4% of the time, Pallas kernels for 42%

profile of v2, /device:TPU:0, one launch (start us, length us, event | category | flops | bytes accessed | tf_op | source)
XLA Modules:
  0.0 160.8 jit_solution(6606015852926546400)
XLA Ops:
  0.6 3.0 %collective-permute-start.2 = (bf16[1,15,15,768]{3,2,1,0:T(8,128)(2,1)}, bf16[1,15,15,768]{3,2,1,0:T(8,128)(2,1)S(1)}, u32[]{:S(2)}, u32[]{:S(2)}) collective-permute-start(bf16[1,15,15,768]{3,2,1,0:T(8,128)(2,1)} %x.3), channel_id=1, source_target_pairs={{0,16},{16,0},{1,17},{17,1},{2,18},{18,2},{3,19},{19,3},{4,20},{20... | collective-permute-start | bytes 1036808 | tf_op jit(solution)/shard_map/ppermute | solution.py:38
  3.7 4.5 %units.1 = (bf16[768,768]{1,0:T(8,128)(2,1)}, f32[1,768]{1,0:T(1,128)}) custom-call(s32[1]{0:T(128)} %bitcast.tile, bf16[768,3072]{1,0:T(8,128)(2,1)} %fc1.3, f32[1,3072]{1,0:T(1,128)} %bitcast.64), custom_call_target="tpu_custom_call" | custom-call | flops 4000000000 | bytes 4000000 | tf_op jit(solution)/shard_map/units/pallas_call | solution.py:538
  8.2 4.1 %heads.1 = (bf16[768,576]{1,0:T(8,128)(2,1)}, f32[1,576]{1,0:T(1,128)}) custom-call(s32[1]{0:T(128)} %bitcast.tile, bf16[768,2304]{1,0:T(8,128)(2,1)} %w.1, f32[2,768]{1,0:T(2,128)} %bitcast.66), custom_call_target="tpu_custom_call" | custom-call | flops 4000000000 | bytes 4000000 | tf_op jit(solution)/shard_map/heads/pallas_call | solution.py:522
  16.4 11.4 %shard_map.254 = (bf16[960,768]{1,0:T(8,128)(2,1)}, bf16[960,768]{1,0:T(8,128)(2,1)}, bf16[960,576]{1,0:T(8,128)(2,1)}, f32[960,128]{1,0:T(8,128)}, bf16[240,192...) custom-call(s32[1]{0:T(128)} %bitcast.tile, ...), custom_call_target="tpu_custom_call" | custom-call | flops 12999999488 | bytes 13000000 | tf_op jit(solution)/shard_map/pallas_call | solution.py:556
  29.7 2.4 %constant_dynamic-slice_fusion.5 = bf16[8,1,96,768]{3,2,1,0:T(8,128)(2,1)} fusion(bf16[8,4,96,768]{3,2,1,0:T(8,128)(2,1)} %bitcast.60, s32[]{:T(128)S(6)} %select_n.69), kind=kLoop, calls=%fused_computation.34 | loop fusion | bytes 2359300 | tf_op jit(solution)/shard_map/jit(dynamic_index_in_dim)/dynamic_slice | solution.py:572
  32.1 2.3 %collective-permute-done.5.c2 = bf16[240,192]{1,0:T(8,128)(2,1)S(1)} collective-permute-done((bf16[240,192]{1,0:T(8,128)(2,1)}, bf16[240,192]{1,0:T(8,128)(2,1)S(1)}, u32[]{:S(2)}, u32[]{:S(2)}) %collective-permute-start.5) | collective-permute-done | bytes 92192 | tf_op jit(solution)/shard_map/ppermute | solution.py:38
  36.5 3.1 %shard_map.255 = (f32[240,768]{1,0:T(8,128)}, bf16[240,768]{1,0:T(8,128)(2,1)}) custom-call(s32[1]{0:T(128)} %bitcast.tile, bf16[240,192]{1,0:T(8,128)(2,1)} %get-tuple-element.128.c0, bf16[240,192]{1,0:T(8,128)(2,1)} %copy-done.35, bf16[240,192]{1,0:T(8,128)(2,1)} %copy-done.36, bf16[240,192]{1,0:T(8,128)(2,1)} %copy-done.37, bf16[768,768]{1,0:T(8,128)(2,1)} %wo.3, ...), custom_call_target="tpu_custom_call" | custom-call | flops 3000000000 | bytes 3000000 | tf_op jit(solution)/shard_map/pallas_call | solution.py:578
  40.4 10.5 %mlp.1 = (bf16[1,15,15,768]{3,2,1,0:T(8,128)(2,1)}, bf16[240,768]{1,0:T(8,128)(2,1)}, f32[240,768]{1,0:T(8,128)}, f32[2,768]{1,0:T(2,128)}) custom-call(s32[1]{0:T(128)} %bitcast.tile, s32[1,30,30]{2,1,0:T(8,128)} %copy.47.mask, f32[240,768]{1,0:T(8,128)} %get-tuple-element.132.resid, bf16[240,768]{1,0:T(8,128)(2,1)} %get-tuple-element.133.hid.h0, ...), custom_call_target="tpu_custom_call" | custom-call | flops 11000000512 | bytes 11000000 | tf_op jit(solution)/shard_map/mlp/pallas_call | solution.py:592
  54.8 9.0 %shard_map.256 = (bf16[768,768]{1,0:T(8,128)(2,1)}, bf16[768,768]{1,0:T(8,128)(2,1)}, f32[1,768]{1,0:T(1,128)}, f32[1,768]{1,0:T(1,128)}) custom-call(s32[1]{0:T(128)} %bitcast.tile, s32[1,30,30]{2,1,0:T(8,128)} %copy.47.mask, bf16[240,768]{1,0:T(8,128)(2,1)} %get-tuple-element.133.hid.h0, bf16[240,768]{1,0:T(8,128)(2,1)} %copy-done.15, ...), custom_call_target="tpu_custom_call" | custom-call | flops 8999999488 | bytes 9000000 | tf_op jit(solution)/shard_map/pallas_call | solution.py:640
  66.3 3.6 %shard_map.257 = (bf16[960,192]{1,0:T(8,128)(2,1)}, bf16[192,768]{1,0:T(8,128)(2,1)}, f32[1,768]{1,0:T(1,128)}) custom-call(s32[1]{0:T(128)} %bitcast.tile, bf16[240,768]{1,0:T(8,128)(2,1)} %get-tuple-element.136.b0, bf16[240,768]{1,0:T(8,128)(2,1)} %copy-done.9, bf16[240,768]{1,0:T(8,128)(2,1)} %copy-done.8, bf16[240,768]{1,0:T(8,128)(2,1)} %copy-done.10, ...), custom_call_target="tpu_custom_call" | custom-call | flops 4000000000 | bytes 4000000 | tf_op jit(solution)/shard_map/pallas_call | solution.py:653
  69.9 1.9 %constant_dynamic-slice_fusion.1 = (bf16[192,192]{1,0:T(8,128)(2,1)S(1)}, bf16[192,192]{1,0:T(8,128)(2,1)S(1)}, bf16[192,192]{1,0:T(8,128)(2,1)S(1)}, bf16[192,192]{1,0:T(8,128)(2,1)}) fusion(bf16[192,768]{1,0:T(8,128)(2,1)} %get-tuple-element.149, s32[]{:T(128)S(6)} %select_n.73, s32[]{:T(128)S(6)} %select_n.72, s32[]{:T(128)S(6)} %select_n.71, s32[]{:T(128)S(6)} %select_n.70), kind=kLoop, calls=%fused_computation.30 | loop fusion | bytes 589840 | tf_op jit(solution)/shard_map/dynamic_slice | solution.py:663
  75.5 3.7 %collective-permute-start.19 = (bf16[2,96,768]{2,1,0:T(8,128)(2,1)S(1)}, bf16[2,96,768]{2,1,0:T(8,128)(2,1)S(1)}, u32[]{:S(2)}, u32[]{:S(2)}) collective-permute-start(bf16[2,96,768]{2,1,0:T(8,128)(2,1)S(1)} %get-tuple-element.218), channel_id=1, source_target_pairs={{0,6},{1,7},{2,4},{3,5},{4,2},{5,3},{6,0},{7,1},{8,14},{9,15},{10,... | collective-permute-start | bytes 884744 | tf_op jit(solution)/shard_map/ppermute | solution.py:95
  80.6 18.3 %shard_map.258 = (bf16[240,576]{1,0:T(8,128)(2,1)}, bf16[240,576]{1,0:T(8,128)(2,1)}, bf16[240,576]{1,0:T(8,128)(2,1)}, bf16[240,576]{1,0:T(8,128)(2,1)}, bf16[7...) custom-call(s32[1]{0:T(128)} %bitcast.tile, s32[1,30,30]{2,1,0:T(8,128)} %copy.47.mask, ...), custom_call_target="tpu_custom_call" | custom-call | flops 17999998976 | bytes 18000000 | tf_op jit(solution)/shard_map/pallas_call | solution.py:674
  102.4 1.6 collective-permute-start.30
  106.9 10.2 %collective-permute-done.18 = bf16[4,98,768]{2,0,1:T(4,128)(2,1)S(1)} collective-permute-done((bf16[4,98,768]{2,0,1:T(4,128)(2,1)S(1)}, bf16[4,98,768]{2,0,1:T(4,128)(2,1)S(1)}, u32[]{:S(2)}, u32[]{:S(2)}) %collective-permute-start.18) | collective-permute-done | bytes 602144 | tf_op jit(solution)/shard_map/ppermute | solution.py:86
  117.1 3.6 %collective-permute-start.26 = (bf16[96,768]{1,0:T(8,128)(2,1)S(1)}, bf16[96,768]{1,0:T(8,128)(2,1)S(1)}, u32[]{:S(2)}, u32[]{:S(2)}) collective-permute-start(bf16[96,768]{1,0:T(8,128)(2,1)S(1)} %get-tuple-element.226), channel_id=1, source_target_pairs={{0,6},{1,7},{2,4},{3,5},{4,2},{5,3},{6,0},{7,1},{8,14},{9,15},{10,... | collective-permute-start | bytes 442376 | tf_op jit(solution)/shard_map/ppermute | solution.py:95
  121.7 3.6 %collective-permute-start.23 = (bf16[98,768]{1,0:T(8,128)(2,1)S(1)}, bf16[98,768]{1,0:T(8,128)(2,1)S(1)}, u32[]{:S(2)}, u32[]{:S(2)}) collective-permute-start(bf16[98,768]{1,0:T(8,128)(2,1)S(1)} %get-tuple-element.222), channel_id=1, source_target_pairs={{0,6},{1,7},{2,4},{3,5},{4,2},{5,3},{6,0},{7,1},{8,14},{9,15},{10,... | collective-permute-start | bytes 451592 | tf_op jit(solution)/shard_map/ppermute | solution.py:95
  125.3 4.9 %shard_map.259 = bf16[1,15,15,768]{3,2,1,0:T(8,128)(2,1)} custom-call(s32[1]{0:T(128)} %bitcast.tile, bf16[240,576]{1,0:T(8,128)(2,1)} %get-tuple-element.178.m0, bf16[240,576]{1,0:T(8,128)(2,1)} %copy-done.23, bf16[240,576]{1,0:T(8,128)(2,1)} %copy-done.24, bf16[240,576]{1,0:T(8,128)(2,1)} %copy-done.25, bf16[768,2304]{1,0:T(8,128)(2,1)} %w.1, ...), custom_call_target="tpu_custom_call" | custom-call | flops 5000000000 | bytes 5000000 | tf_op jit(solution)/shard_map/pallas_call | solution.py:704
  130.3 3.4 %collective-permute-start.25 = (bf16[98,768]{1,0:T(8,128)(2,1)S(1)}, bf16[98,768]{1,0:T(8,128)(2,1)S(1)}, u32[]{:S(2)}, u32[]{:S(2)}) collective-permute-start(bf16[98,768]{1,0:T(8,128)(2,1)S(1)} %get-tuple-element.220), channel_id=1, source_target_pairs={{0,2},{1,3},{2,0},{3,1},{4,6},{5,7},{6,4},{7,5},{8,10},{9,11},{10,... | collective-permute-start | bytes 451592 | tf_op jit(solution)/shard_map/ppermute | solution.py:95
  133.7 5.4 %collective-permute-done.27 = bf16[96,768]{1,0:T(8,128)(2,1)S(1)} collective-permute-done((bf16[96,768]{1,0:T(8,128)(2,1)S(1)}, bf16[96,768]{1,0:T(8,128)(2,1)S(1)}, u32[]{:S(2)}, u32[]{:S(2)}) %collective-permute-start.27) | collective-permute-done | bytes 147488 | tf_op jit(solution)/shard_map/ppermute | solution.py:95
  141.3 3.0 %collective-permute-done.33.p2 = bf16[96,768]{1,0:T(8,128)(2,1)S(1)} collective-permute-done((bf16[96,768]{1,0:T(8,128)(2,1)S(1)}, bf16[96,768]{1,0:T(8,128)(2,1)S(1)}, u32[]{:S(2)}, u32[]{:S(2)}) %collective-permute-start.33) | collective-permute-done | bytes 147488 | tf_op jit(solution)/shard_map/ppermute | solution.py:38
  148.6 2.7 %shard_map.260 = f32[96,3072]{1,0:T(8,128)} custom-call(s32[1]{0:T(128)} %bitcast.tile, bf16[96,768]{1,0:T(8,128)(2,1)} %copy-done.4, bf16[96,768]{1,0:T(8,128)(2,1)} %copy-done.33, bf16[96,768]{1,0:T(8,128)(2,1)} %copy-done.31, bf16[96,768]{1,0:T(8,128)(2,1)} %copy-done.34), custom_call_target="tpu_custom_call" | custom-call | flops 2000000000 | bytes 2000000 | tf_op jit(solution)/shard_map/pallas_call | solution.py:730
  152.7 2.3 %shard_map.261 = f32[384,768]{1,0:T(8,128)} custom-call(s32[1]{0:T(128)} %bitcast.tile, bf16[96,768]{1,0:T(8,128)(2,1)} %copy-done.3, bf16[96,768]{1,0:T(8,128)(2,1)} %copy-done.30, bf16[96,768]{1,0:T(8,128)(2,1)} %copy-done.29, bf16[96,768]{1,0:T(8,128)(2,1)} %copy-done.32), custom_call_target="tpu_custom_call" | custom-call | flops 2000000000 | bytes 2000000 | tf_op jit(solution)/shard_map/pallas_call | solution.py:723
  157.1 2.5 %shard_map.262 = (f32[96,2304]{1,0:T(8,128)}, f32[96,768]{1,0:T(8,128)}, f32[96]{0:T(128)}, f32[96]{0:T(128)}, f32[96]{0:T(128)}, /*index=5*/f32[96]{0:T(128)}, ...) custom-call(s32[1]{0:T(128)} %bitcast.tile, bf16[98,768]{1,0:T(8,128)(2,1)} %copy-done.2, ...), custom_call_target="tpu_custom_call" | custom-call | flops 3000000000 | bytes 3000000 | tf_op jit(solution)/shard_map/pallas_call | solution.py:738
  (171 shorter events, 38.7 us)
Async XLA Ops:
  0.6 11.8 %collective-permute-start.2 = (bf16[1,15,15,768]{3,2,1,0:T(8,128)(2,1)}, bf16[1,15,15,768]{3,2,1,0:T(8,128)(2,1)S(1)}, u32[]{:S(2)}, u32[]{:S(2)}) collective-permute-start(bf16[1,15,15,768]{3,2,1,0:T(8,128)(2,1)} %x.3), channel_id=1, source_target_pairs={{0,16},{16,0},{1,17},{17,1},{2,18},{18,2},{3,19},{19,3},{4,20},{20... | collective-permute-start | bytes 1036808 | tf_op jit(solution)/shard_map/ppermute | solution.py:38
  3.7 11.2 %collective-permute-start.1 = (bf16[1,15,15,768]{3,2,1,0:T(8,128)(2,1)}, bf16[1,15,15,768]{3,2,1,0:T(8,128)(2,1)S(1)}, u32[]{:S(2)}, u32[]{:S(2)}) collective-permute-start(bf16[1,15,15,768]{3,2,1,0:T(8,128)(2,1)} %x.3), channel_id=1, source_target_pairs={{0,8},{8,0},{1,9},{9,1},{2,10},{10,2},{3,11},{11,3},{4,12},{12,4},... | collective-permute-start | bytes 1036808 | tf_op jit(solution)/shard_map/ppermute | solution.py:36
  12.9 14.8 %collective-permute-start = (bf16[1,15,15,768]{3,2,1,0:T(8,128)(2,1)S(1)}, bf16[1,15,15,768]{3,2,1,0:T(8,128)(2,1)S(1)}, u32[]{:S(2)}, u32[]{:S(2)}) collective-permute-start(bf16[1,15,15,768]{3,2,1,0:T(8,128)(2,1)S(1)} %copy-done.6), channel_id=1, source_target_pairs={{0,16},{16,0},{1,17},{17,1},{2,18},{18,2},{3,19},{19,3},{4,20},{20... | collective-permute-start | bytes 1036808 | tf_op jit(solution)/shard_map/ppermute | solution.py:38
  39.6 11.3 %collective-permute-start.7 = (bf16[240,768]{1,0:T(8,128)(2,1)}, bf16[240,768]{1,0:T(8,128)(2,1)S(1)}, u32[]{:S(2)}, u32[]{:S(2)}) collective-permute-start(bf16[240,768]{1,0:T(8,128)(2,1)} %get-tuple-element.133.hid.h0), channel_id=1, source_target_pairs={{0,16},{16,0},{1,17},{17,1},{2,18},{18,2},{3,19},{19,3},{4,20},{20... | collective-permute-start | bytes 1105928 | tf_op jit(solution)/shard_map/ppermute | solution.py:38
  40.4 13.5 %collective-permute-start.10 = (bf16[240,768]{1,0:T(8,128)(2,1)}, bf16[240,768]{1,0:T(8,128)(2,1)S(1)}, u32[]{:S(2)}, u32[]{:S(2)}) collective-permute-start(bf16[240,768]{1,0:T(8,128)(2,1)} %get-tuple-element.133.hid.h0), channel_id=1, source_target_pairs={{0,8},{8,0},{1,9},{9,1},{2,10},{10,2},{3,11},{11,3},{4,12},{12,4},... | collective-permute-start | bytes 1105928 | tf_op jit(solution)/shard_map/ppermute | solution.py:36
  52.0 11.9 %collective-permute-start.9 = (bf16[240,768]{1,0:T(8,128)(2,1)}, bf16[240,768]{1,0:T(8,128)(2,1)S(1)}, u32[]{:S(2)}, u32[]{:S(2)}) collective-permute-start(bf16[240,768]{1,0:T(8,128)(2,1)} %get-tuple-element.136.b0), channel_id=1, source_target_pairs={{0,16},{16,0},{1,17},{17,1},{2,18},{18,2},{3,19},{19,3},{4,20},{20... | collective-permute-start | bytes 1105928 | tf_op jit(solution)/shard_map/ppermute | solution.py:38
  53.3 11.0 %collective-permute-start.8 = (bf16[240,768]{1,0:T(8,128)(2,1)}, bf16[240,768]{1,0:T(8,128)(2,1)S(1)}, u32[]{:S(2)}, u32[]{:S(2)}) collective-permute-start(bf16[240,768]{1,0:T(8,128)(2,1)} %get-tuple-element.136.b0), channel_id=1, source_target_pairs={{0,8},{8,0},{1,9},{9,1},{2,10},{10,2},{3,11},{11,3},{4,12},{12,4},... | collective-permute-start | bytes 1105928 | tf_op jit(solution)/shard_map/ppermute | solution.py:36
  73.8 27.6 %collective-permute-start.22 = (bf16[4,96,768]{2,1,0:T(8,128)(2,1)S(1)}, bf16[4,96,768]{2,1,0:T(8,128)(2,1)S(1)}, u32[]{:S(2)}, u32[]{:S(2)}) collective-permute-start(bf16[4,96,768]{2,1,0:T(8,128)(2,1)S(1)} %get-tuple-element.214), channel_id=1, source_target_pairs={{0,1},{1,0},{2,3},{3,2},{4,5},{5,4},{6,7},{7,6},{8,9},{9,8},{10,11... | collective-permute-start | bytes 1769480 | tf_op jit(solution)/shard_map/ppermute | solution.py:86
  75.5 26.2 %collective-permute-start.19 = (bf16[2,96,768]{2,1,0:T(8,128)(2,1)S(1)}, bf16[2,96,768]{2,1,0:T(8,128)(2,1)S(1)}, u32[]{:S(2)}, u32[]{:S(2)}) collective-permute-start(bf16[2,96,768]{2,1,0:T(8,128)(2,1)S(1)} %get-tuple-element.218), channel_id=1, source_target_pairs={{0,6},{1,7},{2,4},{3,5},{4,2},{5,3},{6,0},{7,1},{8,14},{9,15},{10,... | collective-permute-start | bytes 884744 | tf_op jit(solution)/shard_map/ppermute | solution.py:95
  79.1 25.6 %collective-permute-start.20 = (bf16[2,96,768]{2,1,0:T(8,128)(2,1)S(1)}, bf16[2,96,768]{2,1,0:T(8,128)(2,1)S(1)}, u32[]{:S(2)}, u32[]{:S(2)}) collective-permute-start(bf16[2,96,768]{2,1,0:T(8,128)(2,1)S(1)} %get-tuple-element.217), channel_id=1, source_target_pairs={{0,4},{1,5},{2,6},{3,7},{4,0},{5,1},{6,2},{7,3},{8,12},{9,13},{10,... | collective-permute-start | bytes 884744 | tf_op jit(solution)/shard_map/ppermute | solution.py:95
  79.2 26.0 %collective-permute-start.21 = (bf16[2,96,768]{2,1,0:T(8,128)(2,1)S(1)}, bf16[2,96,768]{2,1,0:T(8,128)(2,1)}, u32[]{:S(2)}, u32[]{:S(2)}) collective-permute-start(bf16[2,96,768]{2,1,0:T(8,128)(2,1)S(1)} %get-tuple-element.216), channel_id=1, source_target_pairs={{0,2},{1,3},{2,0},{3,1},{4,6},{5,7},{6,4},{7,5},{8,10},{9,11},{10,... | collective-permute-start | bytes 884744 | tf_op jit(solution)/shard_map/ppermute | solution.py:95
  100.5 16.5 %collective-permute-start.18 = (bf16[4,98,768]{2,0,1:T(4,128)(2,1)S(1)}, bf16[4,98,768]{2,0,1:T(4,128)(2,1)S(1)}, u32[]{:S(2)}, u32[]{:S(2)}) collective-permute-start(bf16[4,98,768]{2,0,1:T(4,128)(2,1)S(1)} %bitcast.59), channel_id=1, source_target_pairs={{0,1},{1,0},{2,3},{3,2},{4,5},{5,4},{6,7},{7,6},{8,9},{9,8},{10,11... | collective-permute-start | bytes 1806344 | tf_op jit(solution)/shard_map/ppermute | solution.py:86
  101.4 19.5 %collective-permute-start.29 = (bf16[240,576]{1,0:T(8,128)(2,1)S(1)}, bf16[240,576]{1,0:T(8,128)(2,1)S(1)}, u32[]{:S(2)}, u32[]{:S(2)}) collective-permute-start(bf16[240,576]{1,0:T(8,128)(2,1)S(1)} %copy-done.22), channel_id=1, source_target_pairs={{0,8},{8,0},{1,9},{9,1},{2,10},{10,2},{3,11},{11,3},{4,12},{12,4},... | collective-permute-start | bytes 829448 | tf_op jit(solution)/shard_map/ppermute | solution.py:36
  102.4 18.6 %collective-permute-start.30 = (bf16[240,576]{1,0:T(8,128)(2,1)S(1)}, bf16[240,576]{1,0:T(8,128)(2,1)S(1)}, u32[]{:S(2)}, u32[]{:S(2)}) collective-permute-start(bf16[240,576]{1,0:T(8,128)(2,1)S(1)} %copy-done.21), channel_id=1, source_target_pairs={{0,16},{16,0},{1,17},{17,1},{2,18},{18,2},{3,19},{19,3},{4,20},{20... | collective-permute-start | bytes 829448 | tf_op jit(solution)/shard_map/ppermute | solution.py:38
  104.8 16.9 %collective-permute-start.31 = (bf16[240,576]{1,0:T(8,128)(2,1)S(1)}, bf16[240,576]{1,0:T(8,128)(2,1)S(1)}, u32[]{:S(2)}, u32[]{:S(2)}) collective-permute-start(bf16[240,576]{1,0:T(8,128)(2,1)S(1)} %copy-done.20), channel_id=1, source_target_pairs={{0,24},{8,16},{16,8},{24,0},{1,25},{9,17},{17,9},{25,1},{2,26},{10... | collective-permute-start | bytes 829448 | tf_op jit(solution)/shard_map/ppermute | solution.py:39
  106.3 23.9 %collective-permute-start.32 = (bf16[1,96,768]{2,1,0:T(8,128)(2,1)S(1)}, bf16[1,96,768]{2,1,0:T(8,128)(2,1)S(1)}, u32[]{:S(2)}, u32[]{:S(2)}) collective-permute-start(bf16[1,96,768]{2,1,0:T(8,128)(2,1)S(1)} %constant_dynamic-slice_fusion), channel_id=1, source_target_pairs={{0,1},{1,0},{2,3},{3,2},{4,5},{5,4},{6,7},{7,6},{8,9},{9,8},{10,11... | collective-permute-start | bytes 442376 | tf_op jit(solution)/shard_map/ppermute | solution.py:86
  117.1 13.3 %collective-permute-start.26 = (bf16[96,768]{1,0:T(8,128)(2,1)S(1)}, bf16[96,768]{1,0:T(8,128)(2,1)S(1)}, u32[]{:S(2)}, u32[]{:S(2)}) collective-permute-start(bf16[96,768]{1,0:T(8,128)(2,1)S(1)} %get-tuple-element.226), channel_id=1, source_target_pairs={{0,6},{1,7},{2,4},{3,5},{4,2},{5,3},{6,0},{7,1},{8,14},{9,15},{10,... | collective-permute-start | bytes 442376 | tf_op jit(solution)/shard_map/ppermute | solution.py:95
  120.9 18.2 %collective-permute-start.27 = (bf16[96,768]{1,0:T(8,128)(2,1)S(1)}, bf16[96,768]{1,0:T(8,128)(2,1)S(1)}, u32[]{:S(2)}, u32[]{:S(2)}) collective-permute-start(bf16[96,768]{1,0:T(8,128)(2,1)S(1)} %get-tuple-element.225), channel_id=1, source_target_pairs={{0,4},{1,5},{2,6},{3,7},{4,0},{5,1},{6,2},{7,3},{8,12},{9,13},{10,... | collective-permute-start | bytes 442376 | tf_op jit(solution)/shard_map/ppermute | solution.py:95
  121.0 19.4 %collective-permute-start.28 = (bf16[96,768]{1,0:T(8,128)(2,1)S(1)}, bf16[96,768]{1,0:T(8,128)(2,1)S(1)}, u32[]{:S(2)}, u32[]{:S(2)}) collective-permute-start(bf16[96,768]{1,0:T(8,128)(2,1)S(1)} %get-tuple-element.224), channel_id=1, source_target_pairs={{0,2},{1,3},{2,0},{3,1},{4,6},{5,7},{6,4},{7,5},{8,10},{9,11},{10,... | collective-permute-start | bytes 442376 | tf_op jit(solution)/shard_map/ppermute | solution.py:95
  121.7 22.5 %collective-permute-start.23 = (bf16[98,768]{1,0:T(8,128)(2,1)S(1)}, bf16[98,768]{1,0:T(8,128)(2,1)S(1)}, u32[]{:S(2)}, u32[]{:S(2)}) collective-permute-start(bf16[98,768]{1,0:T(8,128)(2,1)S(1)} %get-tuple-element.222), channel_id=1, source_target_pairs={{0,6},{1,7},{2,4},{3,5},{4,2},{5,3},{6,0},{7,1},{8,14},{9,15},{10,... | collective-permute-start | bytes 451592 | tf_op jit(solution)/shard_map/ppermute | solution.py:95
  130.3 14.5 %collective-permute-start.24 = (bf16[98,768]{1,0:T(8,128)(2,1)S(1)}, bf16[98,768]{1,0:T(8,128)(2,1)S(1)}, u32[]{:S(2)}, u32[]{:S(2)}) collective-permute-start(bf16[98,768]{1,0:T(8,128)(2,1)S(1)} %get-tuple-element.221), channel_id=1, source_target_pairs={{0,4},{1,5},{2,6},{3,7},{4,0},{5,1},{6,2},{7,3},{8,12},{9,13},{10,... | collective-permute-start | bytes 451592 | tf_op jit(solution)/shard_map/ppermute | solution.py:95
  130.3 14.5 %collective-permute-start.25 = (bf16[98,768]{1,0:T(8,128)(2,1)S(1)}, bf16[98,768]{1,0:T(8,128)(2,1)S(1)}, u32[]{:S(2)}, u32[]{:S(2)}) collective-permute-start(bf16[98,768]{1,0:T(8,128)(2,1)S(1)} %get-tuple-element.220), channel_id=1, source_target_pairs={{0,2},{1,3},{2,0},{3,1},{4,6},{5,7},{6,4},{7,5},{8,10},{9,11},{10,... | collective-permute-start | bytes 451592 | tf_op jit(solution)/shard_map/ppermute | solution.py:95
  145.9 9.0 %collective-permute-start.35 = (bf16[98,768]{1,0:T(8,128)(2,1)S(1)}, bf16[98,768]{1,0:T(8,128)(2,1)S(1)}, u32[]{:S(2)}, u32[]{:S(2)}) collective-permute-start(bf16[98,768]{1,0:T(8,128)(2,1)S(1)} %add_convert_fusion.3.p0), channel_id=1, source_target_pairs={{0,16},{16,0},{1,17},{17,1},{2,18},{18,2},{3,19},{19,3},{4,20},{20... | collective-permute-start | bytes 451592 | tf_op jit(solution)/shard_map/ppermute | solution.py:38
  147.3 7.9 %collective-permute-start.34 = (bf16[98,768]{1,0:T(8,128)(2,1)S(1)}, bf16[98,768]{1,0:T(8,128)(2,1)S(1)}, u32[]{:S(2)}, u32[]{:S(2)}) collective-permute-start(bf16[98,768]{1,0:T(8,128)(2,1)S(1)} %add_convert_fusion.3.p0), channel_id=1, source_target_pairs={{0,8},{8,0},{1,9},{9,1},{2,10},{10,2},{3,11},{11,3},{4,12},{12,4},... | collective-permute-start | bytes 451592 | tf_op jit(solution)/shard_map/ppermute | solution.py:36
  (59 other events, 225.9 us)

commit v3 on v2

--- a/solution.py
+++ b/solution.py
@@ -113,8 +113,8 @@
 PAD = 16
 
 
-def vec_call(kernel, outs, n_in, scratch=(), us=5):
-    return pl.pallas_call(
+def vec_call(kernel, outs, n_in, scratch=(), us=5, near=()):
+    call = pl.pallas_call(
         kernel,
         out_shape=outs,
         in_specs=[SMEM] + [VMEM] * n_in,
@@ -122,6 +122,15 @@
         scratch_shapes=list(scratch),
         cost_estimate=cost(us),
     )
+
+    def run(*args):
+        placed = [
+            pltpu.with_memory_space_constraint(a, pltpu.VMEM) if i in near else a
+            for i, a in enumerate(args)
+        ]
+        return call(*placed)
+
+    return run
 
 
 def cost(us):
@@ -565,6 +574,7 @@
         9,
         [pltpu.VMEM((total, width), BF), pltpu.VMEM((4, toks, part), BF)],
         us=13,
+        near=(3, 4, 5),
     )(at_tile, patch_mask, *x_blocks, norm1_gain, norm1_shift, w_own, b_own)
     ct_blocks, ctx = gather_tiles(cotangent, ctx)
     later_tile, _ = tie(at_tile, ctx)
@@ -581,6 +591,7 @@
         9,
         [pltpu.VMEM((toks, width), BF)],
         us=3,
+        near=(2, 3, 4),
     )(at_tile, *ctx_in, out_weight, out_bias, patches, norm2_gain, norm2_shift)
 
     chunks = 4
@@ -647,6 +658,7 @@
             pltpu.VMEM((units, width), F32),
         ],
         us=9,
+        near=(3, 4, 5),
     )(at_tile, patch_mask, *hid2_blocks, *ct_blocks, fc1_own, fc1_b_own, fc2_own)
     branch_blocks, (g1, g2) = gather_tiles(branch, (g1, g2))
 
@@ -655,6 +667,7 @@
         [sds((total, part)), sds((part, width)), sds((1, width), F32)],
         9,
         us=4,
+        near=(2, 3, 4),
     )(at_tile, *branch_blocks, out_weight, *ctx)
     direct = direct_sum(imgs)
     (g1, g2), (gout,) = tie((g1, g2), (gout,))
@@ -707,6 +720,7 @@
         8,
         [pltpu.VMEM((4, toks, 3 * part), BF), pltpu.VMEM((toks, width), BF)],
         us=5,
+        near=(2, 3, 4),
     )(at_tile, *mixed_in, qkv_weight, patches, rgrad, norm1_gain)
 
     if direct:
@@ -726,6 +740,7 @@
         4,
         [pltpu.VMEM((4, quarter, width), F32)],
         us=2,
+        near=(2, 3, 4),
     )(at_tile, *fc2_pieces)
     fc1_grad = vec_call(
         functools.partial(fc1out_kernel, quarter=quarter),
@@ -733,6 +748,7 @@
         4,
         [pltpu.VMEM((4, share, units), F32)],
         us=2,
+        near=(2, 3, 4),
     )(at_tile, *fc1_pieces)
     at_pieces, (fc1_grad, fc2_grad) = gather_tiles(at_sum, (fc1_grad, fc2_grad))
     qkv_grad, out_grad, *vec_sums, unit_sum = vec_call(
@@ -746,6 +762,7 @@
         4,
         [pltpu.VMEM((4, share + vec_height, width), F32)],
         us=3,
+        near=(2, 3, 4),
     )(at_tile, *at_pieces)
     return (
         layer_out,

time: 161 us -> 156 us (0.969)
  local copies, waits for them, and re-layouts: 13.7 us -> 9 us
  waiting for transfers between devices: 27 us -> 30 us
  Pallas kernels: 77.1 us -> 75.1 us
    unnamed x83 -> x35, local copies, waits for them, and re-layouts: 8.94 us -> 2.68 us
    pallas_call x9, Pallas kernels: 57.9 us -> 55.9 us  [run(): return call(*placed)]
  transfers between devices with their start and end apart: 42 -> 42, of which waited for: 11 -> 15; matrix products, arithmetic and copies ran while one was open for 4% -> 5% of each run, Pallas kernels for 42% -> 43%
where the time goes in v3:
time: 156 us; the launch traced here: 155 us
  Pallas kernels  75.1 us (48%)
  starting transfers between devices  36.9 us (24%)
  waiting for transfers between devices  30 us (19%)
  local copies, waits for them, and re-layouts  9 us (6%)
  other arithmetic  3.25 us (2%)
    pallas_call x9, Pallas kernels, run(): return call(*placed)  55.9 us
    ppermute x9, starting transfers between devices, exchange_far(): lax.ppermute(send, 'imgs', [(i, i ^ 2 * k) for i in range(count)])  16.3 us
    ppermute x10, starting transfers between devices, to_peer(): return lax.ppermute(value, 'rows', [(0, 1), (1, 0)])  12.2 us
    ppermute x3, waiting for transfers between devices, exchange_near(): lax.ppermute(send, 'imgs', [(i, i ^ 1) for i in range(count)])  11.3 us
    pallas_call x1, Pallas kernels, layer(): pl.pallas_call(mlp_kernel, grid=(chunks,), in_specs=[SMEM, whole(*patch_m...  10.5 us
    ppermute x10, waiting for transfers between devices, to_peer(): return lax.ppermute(value, 'rows', [(0, 1), (1, 0)])  7.18 us
    ppermute x9, waiting for transfers between devices, exchange_far(): lax.ppermute(send, 'imgs', [(i, i ^ 2 * k) for i in range(count)])  6.63 us
    pallas_call x1, Pallas kernels, layer(): pl.pallas_call(functools.partial(units_kernel, quarter=quarter), grid=(st...  4.55 us
  transfers between devices with their start and end apart: 42, of which 15 were waited for; matrix products, arithmetic and copies ran while one was open for 5% of the time, Pallas kernels for 43%

profile of v3, /device:TPU:0, one launch (start us, length us, event | category | flops | bytes accessed | tf_op | source)
XLA Modules:
  0.0 155.1 jit_solution(8776279163446514493)
XLA Ops:
  0.6 3.0 %collective-permute-start.2 = (bf16[1,15,15,768]{3,2,1,0:T(8,128)(2,1)}, bf16[1,15,15,768]{3,2,1,0:T(8,128)(2,1)S(1)}, u32[]{:S(2)}, u32[]{:S(2)}) collective-permute-start(bf16[1,15,15,768]{3,2,1,0:T(8,128)(2,1)} %x.3), channel_id=1, source_target_pairs={{0,16},{16,0},{1,17},{17,1},{2,18},{18,2},{3,19},{19,3},{4,20},{20... | collective-permute-start | bytes 1036808 | tf_op jit(solution)/shard_map/ppermute | solution.py:38
  3.7 4.5 %units.1 = (bf16[768,768]{1,0:T(8,128)(2,1)}, f32[1,768]{1,0:T(1,128)}) custom-call(s32[1]{0:T(128)} %bitcast.tile, bf16[768,3072]{1,0:T(8,128)(2,1)} %fc1.3, f32[1,3072]{1,0:T(1,128)} %bitcast.64), custom_call_target="tpu_custom_call" | custom-call | flops 4000000000 | bytes 4000000 | tf_op jit(solution)/shard_map/units/pallas_call | solution.py:547
  8.2 4.1 %heads.1 = (bf16[768,576]{1,0:T(8,128)(2,1)}, f32[1,576]{1,0:T(1,128)}) custom-call(s32[1]{0:T(128)} %bitcast.tile, bf16[768,2304]{1,0:T(8,128)(2,1)} %w.1, f32[2,768]{1,0:T(2,128)} %bitcast.66), custom_call_target="tpu_custom_call" | custom-call | flops 4000000000 | bytes 4000000 | tf_op jit(solution)/shard_map/heads/pallas_call | solution.py:531
  14.8 11.1 %shard_map.254 = (bf16[960,768]{1,0:T(8,128)(2,1)}, bf16[960,768]{1,0:T(8,128)(2,1)}, bf16[960,576]{1,0:T(8,128)(2,1)}, f32[960,128]{1,0:T(8,128)}, bf16[240,192...) custom-call(s32[1]{0:T(128)} %bitcast.tile, ...), custom_call_target="tpu_custom_call" | custom-call | flops 12999999488 | bytes 13000000 | tf_op jit(solution)/shard_map/pallas_call | solution.py:131
  27.8 2.4 %constant_dynamic-slice_fusion.5 = bf16[8,1,96,768]{3,2,1,0:T(8,128)(2,1)} fusion(bf16[8,4,96,768]{3,2,1,0:T(8,128)(2,1)} %bitcast.60, s32[]{:T(128)S(6)} %select_n.69), kind=kLoop, calls=%fused_computation.34 | loop fusion | bytes 2359300 | tf_op jit(solution)/shard_map/jit(dynamic_index_in_dim)/dynamic_slice | solution.py:582
  30.2 2.4 %collective-permute-done.5.c2 = bf16[240,192]{1,0:T(8,128)(2,1)S(1)} collective-permute-done((bf16[240,192]{1,0:T(8,128)(2,1)}, bf16[240,192]{1,0:T(8,128)(2,1)S(1)}, u32[]{:S(2)}, u32[]{:S(2)}) %collective-permute-start.5) | collective-permute-done | bytes 92192 | tf_op jit(solution)/shard_map/ppermute | solution.py:38
  33.9 2.9 %shard_map.255 = (f32[240,768]{1,0:T(8,128)}, bf16[240,768]{1,0:T(8,128)(2,1)}) custom-call(s32[1]{0:T(128)} %bitcast.tile, bf16[240,192]{1,0:T(8,128)(2,1)} %get-tuple-element.128.c0, bf16[240,192]{1,0:T(8,128)(2,1)S(1)} %collective-permute-done.4.c1, bf16[240,192]{1,0:T(8,128)(2,1)S(1)} %collective-permute-done.5.c2, ...), custom_call_target="tpu_custom_call" | custom-call | flops 3000000000 | bytes 3000000 | tf_op jit(solution)/shard_map/pallas_call | solution.py:131
  38.1 10.5 %mlp.1 = (bf16[1,15,15,768]{3,2,1,0:T(8,128)(2,1)}, bf16[240,768]{1,0:T(8,128)(2,1)}, f32[240,768]{1,0:T(8,128)}, f32[2,768]{1,0:T(2,128)}) custom-call(s32[1]{0:T(128)} %bitcast.tile, s32[1,30,30]{2,1,0:T(8,128)} %copy.47.mask, f32[240,768]{1,0:T(8,128)} %get-tuple-element.132.resid, bf16[240,768]{1,0:T(8,128)(2,1)} %get-tuple-element.133.hid.h0, ...), custom_call_target="tpu_custom_call" | custom-call | flops 11000000512 | bytes 11000000 | tf_op jit(solution)/shard_map/mlp/pallas_call | solution.py:603
  52.2 8.8 %shard_map.256 = (bf16[768,768]{1,0:T(8,128)(2,1)}, bf16[768,768]{1,0:T(8,128)(2,1)}, f32[1,768]{1,0:T(1,128)}, f32[1,768]{1,0:T(1,128)}) custom-call(s32[1]{0:T(128)} %bitcast.tile, s32[1,30,30]{2,1,0:T(8,128)} %copy.47.mask, bf16[240,768]{1,0:T(8,128)(2,1)} %get-tuple-element.133.hid.h0, bf16[240,768]{1,0:T(8,128)(2,1)S(1)} %collective-permute-done.10.h1, ...), custom_call_target="tpu_custom_call" | custom-call | flops 8999999488 | bytes 9000000 | tf_op jit(solution)/shard_map/pallas_call | solution.py:131
  62.7 3.3 %shard_map.257 = (bf16[960,192]{1,0:T(8,128)(2,1)}, bf16[192,768]{1,0:T(8,128)(2,1)}, f32[1,768]{1,0:T(1,128)}) custom-call(s32[1]{0:T(128)} %bitcast.tile, bf16[240,768]{1,0:T(8,128)(2,1)} %get-tuple-element.136.b0, bf16[240,768]{1,0:T(8,128)(2,1)S(1)} %collective-permute-done.8.b1, bf16[240,768]{1,0:T(8,128)(2,1)S(1)} %collective-permute-done.9.b2, ...), custom_call_target="tpu_custom_call" | custom-call | flops 4000000000 | bytes 4000000 | tf_op jit(solution)/shard_map/pallas_call | solution.py:131
  66.0 1.9 %constant_dynamic-slice_fusion.1 = (bf16[192,192]{1,0:T(8,128)(2,1)S(1)}, bf16[192,192]{1,0:T(8,128)(2,1)S(1)}, bf16[192,192]{1,0:T(8,128)(2,1)S(1)}, bf16[192,192]{1,0:T(8,128)(2,1)}) fusion(bf16[192,768]{1,0:T(8,128)(2,1)} %get-tuple-element.149, s32[]{:T(128)S(6)} %select_n.73, s32[]{:T(128)S(6)} %select_n.72, s32[]{:T(128)S(6)} %select_n.71, s32[]{:T(128)S(6)} %select_n.70), kind=kLoop, calls=%fused_computation.30 | loop fusion | bytes 589840 | tf_op jit(solution)/shard_map/dynamic_slice | solution.py:676
  70.6 1.5 collective-permute-start.22
  72.3 3.7 %collective-permute-start.19 = (bf16[2,96,768]{2,1,0:T(8,128)(2,1)S(1)}, bf16[2,96,768]{2,1,0:T(8,128)(2,1)S(1)}, u32[]{:S(2)}, u32[]{:S(2)}) collective-permute-start(bf16[2,96,768]{2,1,0:T(8,128)(2,1)S(1)} %get-tuple-element.218), channel_id=1, source_target_pairs={{0,6},{1,7},{2,4},{3,5},{4,2},{5,3},{6,0},{7,1},{8,14},{9,15},{10,... | collective-permute-start | bytes 884744 | tf_op jit(solution)/shard_map/ppermute | solution.py:95
  78.0 18.3 %shard_map.258 = (bf16[240,576]{1,0:T(8,128)(2,1)}, bf16[240,576]{1,0:T(8,128)(2,1)}, bf16[240,576]{1,0:T(8,128)(2,1)}, bf16[240,576]{1,0:T(8,128)(2,1)}, bf16[7...) custom-call(s32[1]{0:T(128)} %bitcast.tile, s32[1,30,30]{2,1,0:T(8,128)} %copy.47.mask, ...), custom_call_target="tpu_custom_call" | custom-call | flops 17999998976 | bytes 18000000 | tf_op jit(solution)/shard_map/pallas_call | solution.py:131
  103.2 11.3 %collective-permute-done.18 = bf16[4,98,768]{2,0,1:T(4,128)(2,1)S(1)} collective-permute-done((bf16[4,98,768]{2,0,1:T(4,128)(2,1)S(1)}, bf16[4,98,768]{2,0,1:T(4,128)(2,1)S(1)}, u32[]{:S(2)}, u32[]{:S(2)}) %collective-permute-start.18) | collective-permute-done | bytes 602144 | tf_op jit(solution)/shard_map/ppermute | solution.py:86
  114.5 3.6 %collective-permute-start.26 = (bf16[96,768]{1,0:T(8,128)(2,1)}, bf16[96,768]{1,0:T(8,128)(2,1)S(1)}, u32[]{:S(2)}, u32[]{:S(2)}) collective-permute-start(bf16[96,768]{1,0:T(8,128)(2,1)} %get-tuple-element.226), channel_id=1, source_target_pairs={{0,6},{1,7},{2,4},{3,5},{4,2},{5,3},{6,0},{7,1},{8,14},{9,15},{10,... | collective-permute-start | bytes 442376 | tf_op jit(solution)/shard_map/ppermute | solution.py:95
  119.2 3.6 %collective-permute-start.23 = (bf16[98,768]{1,0:T(8,128)(2,1)S(1)}, bf16[98,768]{1,0:T(8,128)(2,1)S(1)}, u32[]{:S(2)}, u32[]{:S(2)}) collective-permute-start(bf16[98,768]{1,0:T(8,128)(2,1)S(1)} %get-tuple-element.222), channel_id=1, source_target_pairs={{0,6},{1,7},{2,4},{3,5},{4,2},{5,3},{6,0},{7,1},{8,14},{9,15},{10,... | collective-permute-start | bytes 451592 | tf_op jit(solution)/shard_map/ppermute | solution.py:95
  122.8 4.6 %shard_map.259 = bf16[1,15,15,768]{3,2,1,0:T(8,128)(2,1)} custom-call(s32[1]{0:T(128)} %bitcast.tile, bf16[240,576]{1,0:T(8,128)(2,1)} %get-tuple-element.178.m0, bf16[240,576]{1,0:T(8,128)(2,1)S(1)} %collective-permute-done.29.m1, bf16[240,576]{1,0:T(8,128)(2,1)S(1)} %collective-permute-done.30.m2, bf16[240,576]{1,0:T(8,128)(2,1)S(1)} %collective-permute-done.31.m3, ...), custom_call_target="tpu_custom_call" | custom-call | flops 5000000000 | bytes 5000000 | tf_op jit(solution)/shard_map/pallas_call | solution.py:131
  127.5 3.8 %collective-permute-start.25 = (bf16[98,768]{1,0:T(8,128)(2,1)S(1)}, bf16[98,768]{1,0:T(8,128)(2,1)S(1)}, u32[]{:S(2)}, u32[]{:S(2)}) collective-permute-start(bf16[98,768]{1,0:T(8,128)(2,1)S(1)} %get-tuple-element.220), channel_id=1, source_target_pairs={{0,2},{1,3},{2,0},{3,1},{4,6},{5,7},{6,4},{7,5},{8,10},{9,11},{10,... | collective-permute-start | bytes 451592 | tf_op jit(solution)/shard_map/ppermute | solution.py:95
  131.3 5.4 %collective-permute-done.27 = bf16[96,768]{1,0:T(8,128)(2,1)S(1)} collective-permute-done((bf16[96,768]{1,0:T(8,128)(2,1)}, bf16[96,768]{1,0:T(8,128)(2,1)S(1)}, u32[]{:S(2)}, u32[]{:S(2)}) %collective-permute-start.27) | collective-permute-done | bytes 147488 | tf_op jit(solution)/shard_map/ppermute | solution.py:95
  138.9 2.9 %collective-permute-done.33.p2 = bf16[96,768]{1,0:T(8,128)(2,1)S(1)} collective-permute-done((bf16[96,768]{1,0:T(8,128)(2,1)S(1)}, bf16[96,768]{1,0:T(8,128)(2,1)S(1)}, u32[]{:S(2)}, u32[]{:S(2)}) %collective-permute-start.33) | collective-permute-done | bytes 147488 | tf_op jit(solution)/shard_map/ppermute | solution.py:38
  144.8 2.5 %shard_map.260 = f32[96,3072]{1,0:T(8,128)} custom-call(s32[1]{0:T(128)} %bitcast.tile, bf16[96,768]{1,0:T(8,128)(2,1)} %copy-done.4, bf16[96,768]{1,0:T(8,128)(2,1)S(1)} %collective-permute-done.36.p1, bf16[96,768]{1,0:T(8,128)(2,1)S(1)} %collective-permute-done.37.p2, bf16[96,768]{1,0:T(8,128)(2,1)S(1)} %collective-permute-done.38.p3), custom_call_target="tpu_custom_call" | custom-call | flops 2000000000 | bytes 2000000 | tf_op jit(solution)/shard_map/pallas_call | solution.py:131
  147.4 2.1 %shard_map.261 = f32[384,768]{1,0:T(8,128)} custom-call(s32[1]{0:T(128)} %bitcast.tile, bf16[96,768]{1,0:T(8,128)(2,1)} %copy-done.3, bf16[96,768]{1,0:T(8,128)(2,1)S(1)} %collective-permute-done.39.p1, bf16[96,768]{1,0:T(8,128)(2,1)S(1)} %collective-permute-done.33.p2, bf16[96,768]{1,0:T(8,128)(2,1)S(1)} %collective-permute-done.40.p3), custom_call_target="tpu_custom_call" | custom-call | flops 2000000000 | bytes 2000000 | tf_op jit(solution)/shard_map/pallas_call | solution.py:131
  151.5 2.3 %shard_map.262 = (f32[96,2304]{1,0:T(8,128)}, f32[96,768]{1,0:T(8,128)}, f32[96]{0:T(128)}, f32[96]{0:T(128)}, f32[96]{0:T(128)}, /*index=5*/f32[96]{0:T(128)}, ...) custom-call(s32[1]{0:T(128)} %bitcast.tile, bf16[98,768]{1,0:T(8,128)(2,1)} %copy-done.2, ...), custom_call_target="tpu_custom_call" | custom-call | flops 3000000000 | bytes 3000000 | tf_op jit(solution)/shard_map/pallas_call | solution.py:131
  (123 shorter events, 33.5 us)
Async XLA Ops:
  0.6 11.8 %collective-permute-start.2 = (bf16[1,15,15,768]{3,2,1,0:T(8,128)(2,1)}, bf16[1,15,15,768]{3,2,1,0:T(8,128)(2,1)S(1)}, u32[]{:S(2)}, u32[]{:S(2)}) collective-permute-start(bf16[1,15,15,768]{3,2,1,0:T(8,128)(2,1)} %x.3), channel_id=1, source_target_pairs={{0,16},{16,0},{1,17},{17,1},{2,18},{18,2},{3,19},{19,3},{4,20},{20... | collective-permute-start | bytes 1036808 | tf_op jit(solution)/shard_map/ppermute | solution.py:38
  3.7 11.2 %collective-permute-start.1 = (bf16[1,15,15,768]{3,2,1,0:T(8,128)(2,1)}, bf16[1,15,15,768]{3,2,1,0:T(8,128)(2,1)S(1)}, u32[]{:S(2)}, u32[]{:S(2)}) collective-permute-start(bf16[1,15,15,768]{3,2,1,0:T(8,128)(2,1)} %x.3), channel_id=1, source_target_pairs={{0,8},{8,0},{1,9},{9,1},{2,10},{10,2},{3,11},{11,3},{4,12},{12,4},... | collective-permute-start | bytes 1036808 | tf_op jit(solution)/shard_map/ppermute | solution.py:36
  12.9 13.1 %collective-permute-start = (bf16[1,15,15,768]{3,2,1,0:T(8,128)(2,1)S(1)}, bf16[1,15,15,768]{3,2,1,0:T(8,128)(2,1)S(1)}, u32[]{:S(2)}, u32[]{:S(2)}) collective-permute-start(bf16[1,15,15,768]{3,2,1,0:T(8,128)(2,1)S(1)} %copy-done.6), channel_id=1, source_target_pairs={{0,16},{16,0},{1,17},{17,1},{2,18},{18,2},{3,19},{19,3},{4,20},{20... | collective-permute-start | bytes 1036808 | tf_op jit(solution)/shard_map/ppermute | solution.py:38
  36.8 11.8 %collective-permute-start.7 = (bf16[240,768]{1,0:T(8,128)(2,1)}, bf16[240,768]{1,0:T(8,128)(2,1)S(1)}, u32[]{:S(2)}, u32[]{:S(2)}) collective-permute-start(bf16[240,768]{1,0:T(8,128)(2,1)} %get-tuple-element.133.hid.h0), channel_id=1, source_target_pairs={{0,16},{16,0},{1,17},{17,1},{2,18},{18,2},{3,19},{19,3},{4,20},{20... | collective-permute-start | bytes 1105928 | tf_op jit(solution)/shard_map/ppermute | solution.py:38
  37.9 13.5 %collective-permute-start.10 = (bf16[240,768]{1,0:T(8,128)(2,1)}, bf16[240,768]{1,0:T(8,128)(2,1)S(1)}, u32[]{:S(2)}, u32[]{:S(2)}) collective-permute-start(bf16[240,768]{1,0:T(8,128)(2,1)} %get-tuple-element.133.hid.h0), channel_id=1, source_target_pairs={{0,8},{8,0},{1,9},{9,1},{2,10},{10,2},{3,11},{11,3},{4,12},{12,4},... | collective-permute-start | bytes 1105928 | tf_op jit(solution)/shard_map/ppermute | solution.py:36
  49.6 11.4 %collective-permute-start.9 = (bf16[240,768]{1,0:T(8,128)(2,1)}, bf16[240,768]{1,0:T(8,128)(2,1)S(1)}, u32[]{:S(2)}, u32[]{:S(2)}) collective-permute-start(bf16[240,768]{1,0:T(8,128)(2,1)} %get-tuple-element.136.b0), channel_id=1, source_target_pairs={{0,16},{16,0},{1,17},{17,1},{2,18},{18,2},{3,19},{19,3},{4,20},{20... | collective-permute-start | bytes 1105928 | tf_op jit(solution)/shard_map/ppermute | solution.py:38
  50.9 10.5 %collective-permute-start.8 = (bf16[240,768]{1,0:T(8,128)(2,1)}, bf16[240,768]{1,0:T(8,128)(2,1)S(1)}, u32[]{:S(2)}, u32[]{:S(2)}) collective-permute-start(bf16[240,768]{1,0:T(8,128)(2,1)} %get-tuple-element.136.b0), channel_id=1, source_target_pairs={{0,8},{8,0},{1,9},{9,1},{2,10},{10,2},{3,11},{11,3},{4,12},{12,4},... | collective-permute-start | bytes 1105928 | tf_op jit(solution)/shard_map/ppermute | solution.py:36
  68.3 8.3 %collective-permute-start.16 = (bf16[192,192]{1,0:T(8,128)(2,1)S(1)}, bf16[192,192]{1,0:T(8,128)(2,1)S(1)}, u32[]{:S(2)}, u32[]{:S(2)}) collective-permute-start(bf16[192,192]{1,0:T(8,128)(2,1)S(1)} %get-tuple-element.229), channel_id=1, source_target_pairs={{0,16},{16,0},{1,17},{17,1},{2,18},{18,2},{3,19},{19,3},{4,20},{20... | collective-permute-start | bytes 221192 | tf_op jit(solution)/shard_map/ppermute | solution.py:38
  69.1 8.2 %collective-permute-start.17 = (bf16[192,192]{1,0:T(8,128)(2,1)S(1)}, bf16[192,192]{1,0:T(8,128)(2,1)S(1)}, u32[]{:S(2)}, u32[]{:S(2)}) collective-permute-start(bf16[192,192]{1,0:T(8,128)(2,1)S(1)} %get-tuple-element.228), channel_id=1, source_target_pairs={{0,24},{8,16},{16,8},{24,0},{1,25},{9,17},{17,9},{25,1},{2,26},{10... | collective-permute-start | bytes 221192 | tf_op jit(solution)/shard_map/ppermute | solution.py:39
  70.6 27.9 %collective-permute-start.22 = (bf16[4,96,768]{2,1,0:T(8,128)(2,1)}, bf16[4,96,768]{2,1,0:T(8,128)(2,1)S(1)}, u32[]{:S(2)}, u32[]{:S(2)}) collective-permute-start(bf16[4,96,768]{2,1,0:T(8,128)(2,1)} %get-tuple-element.214), channel_id=1, source_target_pairs={{0,1},{1,0},{2,3},{3,2},{4,5},{5,4},{6,7},{7,6},{8,9},{9,8},{10,11... | collective-permute-start | bytes 1769480 | tf_op jit(solution)/shard_map/ppermute | solution.py:86
  72.3 27.2 %collective-permute-start.19 = (bf16[2,96,768]{2,1,0:T(8,128)(2,1)S(1)}, bf16[2,96,768]{2,1,0:T(8,128)(2,1)S(1)}, u32[]{:S(2)}, u32[]{:S(2)}) collective-permute-start(bf16[2,96,768]{2,1,0:T(8,128)(2,1)S(1)} %get-tuple-element.218), channel_id=1, source_target_pairs={{0,6},{1,7},{2,4},{3,5},{4,2},{5,3},{6,0},{7,1},{8,14},{9,15},{10,... | collective-permute-start | bytes 884744 | tf_op jit(solution)/shard_map/ppermute | solution.py:95
  76.6 25.0 %collective-permute-start.20 = (bf16[2,96,768]{2,1,0:T(8,128)(2,1)S(1)}, bf16[2,96,768]{2,1,0:T(8,128)(2,1)S(1)}, u32[]{:S(2)}, u32[]{:S(2)}) collective-permute-start(bf16[2,96,768]{2,1,0:T(8,128)(2,1)S(1)} %get-tuple-element.217), channel_id=1, source_target_pairs={{0,4},{1,5},{2,6},{3,7},{4,0},{5,1},{6,2},{7,3},{8,12},{9,13},{10,... | collective-permute-start | bytes 884744 | tf_op jit(solution)/shard_map/ppermute | solution.py:95
  76.6 25.0 %collective-permute-start.21 = (bf16[2,96,768]{2,1,0:T(8,128)(2,1)S(1)}, bf16[2,96,768]{2,1,0:T(8,128)(2,1)S(1)}, u32[]{:S(2)}, u32[]{:S(2)}) collective-permute-start(bf16[2,96,768]{2,1,0:T(8,128)(2,1)S(1)} %get-tuple-element.216), channel_id=1, source_target_pairs={{0,2},{1,3},{2,0},{3,1},{4,6},{5,7},{6,4},{7,5},{8,10},{9,11},{10,... | collective-permute-start | bytes 884744 | tf_op jit(solution)/shard_map/ppermute | solution.py:95
  98.0 16.5 %collective-permute-start.18 = (bf16[4,98,768]{2,0,1:T(4,128)(2,1)S(1)}, bf16[4,98,768]{2,0,1:T(4,128)(2,1)S(1)}, u32[]{:S(2)}, u32[]{:S(2)}) collective-permute-start(bf16[4,98,768]{2,0,1:T(4,128)(2,1)S(1)} %bitcast.59), channel_id=1, source_target_pairs={{0,1},{1,0},{2,3},{3,2},{4,5},{5,4},{6,7},{7,6},{8,9},{9,8},{10,11... | collective-permute-start | bytes 1806344 | tf_op jit(solution)/shard_map/ppermute | solution.py:86
  98.5 19.8 %collective-permute-start.29 = (bf16[240,576]{1,0:T(8,128)(2,1)S(1)}, bf16[240,576]{1,0:T(8,128)(2,1)S(1)}, u32[]{:S(2)}, u32[]{:S(2)}) collective-permute-start(bf16[240,576]{1,0:T(8,128)(2,1)S(1)} %copy-done.13), channel_id=1, source_target_pairs={{0,8},{8,0},{1,9},{9,1},{2,10},{10,2},{3,11},{11,3},{4,12},{12,4},... | collective-permute-start | bytes 829448 | tf_op jit(solution)/shard_map/ppermute | solution.py:36
  99.5 18.9 %collective-permute-start.30 = (bf16[240,576]{1,0:T(8,128)(2,1)S(1)}, bf16[240,576]{1,0:T(8,128)(2,1)S(1)}, u32[]{:S(2)}, u32[]{:S(2)}) collective-permute-start(bf16[240,576]{1,0:T(8,128)(2,1)S(1)} %copy-done.12), channel_id=1, source_target_pairs={{0,16},{16,0},{1,17},{17,1},{2,18},{18,2},{3,19},{19,3},{4,20},{20... | collective-permute-start | bytes 829448 | tf_op jit(solution)/shard_map/ppermute | solution.py:38
  101.6 17.6 %collective-permute-start.31 = (bf16[240,576]{1,0:T(8,128)(2,1)S(1)}, bf16[240,576]{1,0:T(8,128)(2,1)S(1)}, u32[]{:S(2)}, u32[]{:S(2)}) collective-permute-start(bf16[240,576]{1,0:T(8,128)(2,1)S(1)} %copy-done.11), channel_id=1, source_target_pairs={{0,24},{8,16},{16,8},{24,0},{1,25},{9,17},{17,9},{25,1},{2,26},{10... | collective-permute-start | bytes 829448 | tf_op jit(solution)/shard_map/ppermute | solution.py:39
  101.8 25.7 %collective-permute-start.32 = (bf16[1,96,768]{2,1,0:T(8,128)(2,1)S(1)}, bf16[1,96,768]{2,1,0:T(8,128)(2,1)S(1)}, u32[]{:S(2)}, u32[]{:S(2)}) collective-permute-start(bf16[1,96,768]{2,1,0:T(8,128)(2,1)S(1)} %constant_dynamic-slice_fusion), channel_id=1, source_target_pairs={{0,1},{1,0},{2,3},{3,2},{4,5},{5,4},{6,7},{7,6},{8,9},{9,8},{10,11... | collective-permute-start | bytes 442376 | tf_op jit(solution)/shard_map/ppermute | solution.py:86
  114.5 13.0 %collective-permute-start.26 = (bf16[96,768]{1,0:T(8,128)(2,1)}, bf16[96,768]{1,0:T(8,128)(2,1)S(1)}, u32[]{:S(2)}, u32[]{:S(2)}) collective-permute-start(bf16[96,768]{1,0:T(8,128)(2,1)} %get-tuple-element.226), channel_id=1, source_target_pairs={{0,6},{1,7},{2,4},{3,5},{4,2},{5,3},{6,0},{7,1},{8,14},{9,15},{10,... | collective-permute-start | bytes 442376 | tf_op jit(solution)/shard_map/ppermute | solution.py:95
  118.3 18.4 %collective-permute-start.27 = (bf16[96,768]{1,0:T(8,128)(2,1)}, bf16[96,768]{1,0:T(8,128)(2,1)S(1)}, u32[]{:S(2)}, u32[]{:S(2)}) collective-permute-start(bf16[96,768]{1,0:T(8,128)(2,1)} %get-tuple-element.225), channel_id=1, source_target_pairs={{0,4},{1,5},{2,6},{3,7},{4,0},{5,1},{6,2},{7,3},{8,12},{9,13},{10,... | collective-permute-start | bytes 442376 | tf_op jit(solution)/shard_map/ppermute | solution.py:95
  118.4 19.1 %collective-permute-start.28 = (bf16[96,768]{1,0:T(8,128)(2,1)}, bf16[96,768]{1,0:T(8,128)(2,1)S(1)}, u32[]{:S(2)}, u32[]{:S(2)}) collective-permute-start(bf16[96,768]{1,0:T(8,128)(2,1)} %get-tuple-element.224), channel_id=1, source_target_pairs={{0,2},{1,3},{2,0},{3,1},{4,6},{5,7},{6,4},{7,5},{8,10},{9,11},{10,... | collective-permute-start | bytes 442376 | tf_op jit(solution)/shard_map/ppermute | solution.py:95
  119.2 22.7 %collective-permute-start.23 = (bf16[98,768]{1,0:T(8,128)(2,1)S(1)}, bf16[98,768]{1,0:T(8,128)(2,1)S(1)}, u32[]{:S(2)}, u32[]{:S(2)}) collective-permute-start(bf16[98,768]{1,0:T(8,128)(2,1)S(1)} %get-tuple-element.222), channel_id=1, source_target_pairs={{0,6},{1,7},{2,4},{3,5},{4,2},{5,3},{6,0},{7,1},{8,14},{9,15},{10,... | collective-permute-start | bytes 451592 | tf_op jit(solution)/shard_map/ppermute | solution.py:95
  127.4 15.1 %collective-permute-start.24 = (bf16[98,768]{1,0:T(8,128)(2,1)S(1)}, bf16[98,768]{1,0:T(8,128)(2,1)S(1)}, u32[]{:S(2)}, u32[]{:S(2)}) collective-permute-start(bf16[98,768]{1,0:T(8,128)(2,1)S(1)} %get-tuple-element.221), channel_id=1, source_target_pairs={{0,4},{1,5},{2,6},{3,7},{4,0},{5,1},{6,2},{7,3},{8,12},{9,13},{10,... | collective-permute-start | bytes 451592 | tf_op jit(solution)/shard_map/ppermute | solution.py:95
  127.5 15.0 %collective-permute-start.25 = (bf16[98,768]{1,0:T(8,128)(2,1)S(1)}, bf16[98,768]{1,0:T(8,128)(2,1)S(1)}, u32[]{:S(2)}, u32[]{:S(2)}) collective-permute-start(bf16[98,768]{1,0:T(8,128)(2,1)S(1)} %get-tuple-element.220), channel_id=1, source_target_pairs={{0,2},{1,3},{2,0},{3,1},{4,6},{5,7},{6,4},{7,5},{8,10},{9,11},{10,... | collective-permute-start | bytes 451592 | tf_op jit(solution)/shard_map/ppermute | solution.py:95
  (35 other events, 172.4 us)
